TPU v7x, 32 devices: a whole 2x2x4 slice. The times are simulated.
32 devices in a mesh: rep: 4 (over y, core), tp: 8 (over z, x).
Axes of the slice: x: 2, y: 2, z: 4, core: 2. Of those that a mesh axis runs over, the one named last changes fastest.
Arguments:
- tokens: bfloat16 [4, 192, 6144], P('rep', 'tp'), may hold values from -6 to 6
- cotangent: bfloat16 [4, 192, 6144], P('rep', 'tp'), may hold values from -6 to 6
- w_in: bfloat16 [4, 6144, 12288], P('rep', None, 'tp'), may hold values from -6 to 6
- w_out: bfloat16 [4, 12288, 6144], P('rep', 'tp'), may hold values from -6 to 6
- gossip_step: int32 [1], replicated, may hold values from 0 to 7
Outputs:
- input_grad: bfloat16 [4, 192, 6144], P('rep', 'tp')
- mixed_in: bfloat16 [4, 6144, 12288], P('rep', None, 'tp')
- mixed_out: bfloat16 [4, 12288, 6144], P('rep', 'tp')
All inputs are finite; a program needn't handle non-finite values.
Results may differ from a plain program's by a relative error of at most 0.023.
Values may be sent and summed in bfloat16 or wider, within the bound.
No kernel may reach another device: no remote copies, remote signals or barrier semaphores. Data moves between devices by JAX's collectives and lax.ppermute only.
A program may use at most 256 MiB of HBM per device.

v0:
```python
from functools import partial

import jax
import jax.numpy as jnp
from jax import lax
from jax.experimental import pallas as pl
from jax.experimental.pallas import tpu as pltpu
from jax.sharding import PartitionSpec as P


def from_partner(value, stride):
    mask = 2**stride
    pairs = [(source, source ^ mask) for source in range(lax.axis_size("rep"))]
    return lax.ppermute(value, "rep", pairs)


def after(value, *earlier):
    return lax.optimization_barrier((value, *earlier))[0]


def gelu_parts(preact):
    cdf = 0.5 * (1.0 + lax.erf(preact * 0.7071067811865476))
    dens = jnp.exp(-0.5 * preact * preact) * 0.3989422804014327
    return (preact * cdf, cdf + preact * dens)


def flip_size():
    return 2 if lax.axis_size("tp") % 2 == 0 else 1


def step_up(value):
    size, inner = lax.axis_size("tp"), flip_size()
    return lax.ppermute(value, "tp", [(i, (i + inner) % size) for i in range(size)])


def flip(value):
    return lax.ppermute(value, "tp", [(i, i ^ 1) for i in range(lax.axis_size("tp"))])


def short_ring():
    return lax.axis_size("tp") // flip_size() <= 4


def gather_slots(shard):
    inner = flip_size()
    ring = lax.axis_size("tp") // inner
    straight, flipped, current = [], [], shard
    for step in range(ring):
        if step:
            current = step_up(current)
        straight.append(current)
        if inner == 2:
            flipped.append(flip(current))
    return straight + flipped


def gather_rows(*shards):
    if not short_ring():
        return [lax.all_gather(shard, "tp", axis=0, tiled=True) for shard in shards]
    rows = shards[0].shape[0]
    slots = gather_slots(jnp.concatenate(shards, axis=0) if len(shards) > 1 else shards[0])
    return [
        jnp.concatenate([slot[n * rows : (n + 1) * rows] for slot in slots], axis=0)
        for n in range(len(shards))
    ]


def scatter_sum(partial_sums, rows, pieces=()):
    pieces, given = list(pieces), ()

    def work(gate, *arrived):
        nonlocal given
        if not pieces:
            return arrived
        given = pieces.pop(0)(gate, given)
        arrived, given = lax.optimization_barrier((arrived, given))
        return arrived

    if not short_ring():
        done = lax.psum_scatter(partial_sums, "tp", scatter_dimension=0, tiled=True)
        while pieces:
            work(partial_sums)
        return done, given
    inner = flip_size()
    ring = lax.axis_size("tp") // inner
    slot = lambda number: partial_sums[number * rows : (number + 1) * rows]
    arrived = [None] * ring
    if inner == 2:
        arrived = [flip(slot(ring + (k + 1) % ring)) for k in range(ring)]
        (arrived[0],) = work(partial_sums, arrived[0])
    carried = None
    for k in range(ring):
        total = slot((k + 1) % ring).astype(jnp.float32)
        if arrived[k] is not None:
            total = total + arrived[k].astype(jnp.float32)
        if carried is not None:
            total = total + carried.astype(jnp.float32)
        carried = total.astype(jnp.bfloat16)
        if k < ring - 1:
            (carried,) = work(carried, step_up(carried))
    while pieces:
        work(carried)
    return carried, given


def dot_tn(left, right):
    return lax.dot_general(
        left, right, (((0,), (0,)), ((), ())), preferred_element_type=jnp.float32
    )


def dot_nt(left, right):
    return lax.dot_general(
        left, right, (((1,), (1,)), ((), ())), preferred_element_type=jnp.float32
    )


def mean_of(own, other):
    return ((own.astype(jnp.float32) + other.astype(jnp.float32)) * 0.5).astype(jnp.bfloat16)


def activations(tokens, upstream, w_in, w_out, scale_in, scale_out):
    preact = jnp.dot(tokens, w_in, preferred_element_type=jnp.float32) * scale_in
    value, slope = gelu_parts(preact)
    back = dot_nt(upstream, w_out) * scale_out
    return value.astype(jnp.bfloat16), (back * slope).astype(jnp.bfloat16)


def forward_kernel(*refs, slots, scale_in, scale_out):
    tok_slots, up_slots = refs[:slots], refs[slots : 2 * slots]
    w_in_ref, w_out_ref, hidden_ref, dpre_ref, part_ref, tok_ref, up_ref, acc_ref = refs[2 * slots :]
    step = pl.program_id(0)

    @pl.when(step == 0)
    def _():
        for whole, parts in ((tok_ref, tok_slots), (up_ref, up_slots)):
            rows = parts[0].shape[0]
            for number, part in enumerate(parts):
                whole[number * rows : (number + 1) * rows, :] = part[...]

    preact = jnp.dot(tok_ref[...], w_in_ref[...], preferred_element_type=jnp.float32) * scale_in
    back = dot_nt(up_ref[...], w_out_ref[...]) * scale_out
    value, slope = gelu_parts(preact)
    hidden_ref[...] = value.astype(jnp.bfloat16)
    dpre = (back * slope).astype(jnp.bfloat16)
    dpre_ref[...] = dpre
    part = dot_nt(dpre, w_in_ref[...])

    @pl.when(step == 0)
    def _():
        acc_ref[...] = part

    @pl.when(step > 0)
    def _():
        acc_ref[...] += part

    @pl.when(step == pl.num_programs(0) - 1)
    def _():
        part_ref[...] = (acc_ref[...] * scale_in).astype(jnp.bfloat16)


def forward(tok_slots, up_slots, w_in, w_out, scale_in, scale_out):
    width, hid = w_in.shape
    slots, part_rows = len(tok_slots), tok_slots[0].shape[0]
    rows, cols = slots * part_rows, 256
    if rows > 256 or hid % cols:
        tokens, upstream = jnp.concatenate(tok_slots, axis=0), jnp.concatenate(up_slots, axis=0)
        hidden, dpre = activations(tokens, upstream, w_in, w_out, scale_in, scale_out)
        partials = (dot_nt(dpre, w_in) * scale_in).astype(jnp.bfloat16)
        return hidden, dpre, partials, tokens, upstream
    once = lambda count: pl.BlockSpec((count, width), lambda i: (0, 0), pipeline_mode=pl.Buffered(1))
    block = pl.BlockSpec((rows, cols), lambda i: (0, i))
    wide = jax.ShapeDtypeStruct((rows, width), jnp.bfloat16)
    tall = jax.ShapeDtypeStruct((rows, hid), jnp.bfloat16)
    return pl.pallas_call(
        partial(forward_kernel, slots=slots, scale_in=scale_in, scale_out=scale_out),
        grid=(hid // cols,),
        in_specs=[
            *[once(part_rows)] * (2 * slots),
            pl.BlockSpec((width, cols), lambda i: (0, i)),
            pl.BlockSpec((cols, width), lambda i: (i, 0)),
        ],
        out_specs=[block, block, *[once(rows)] * 3],
        out_shape=[tall, tall, wide, wide, wide],
        scratch_shapes=[pltpu.VMEM((rows, width), jnp.float32)],
        compiler_params=pltpu.CompilerParams(vmem_limit_bytes=52 << 20),
        cost_estimate=pl.CostEstimate(
            flops=6 * rows * width * hid, bytes_accessed=4 * width * hid, transcendentals=2 * rows * hid
        ),
        name="forward",
    )(*tok_slots, *up_slots, w_in, w_out)


def finish_kernel(factor_ref, own_ref, other_ref, left_ref, left2_ref, right_ref, right2_ref, *out_refs):
    grad = dot_tn(left_ref[...], right_ref[...]) + dot_tn(left2_ref[...], right2_ref[...])
    both = own_ref[...].astype(jnp.float32) + other_ref[...].astype(jnp.float32)
    out_refs[-1][...] = (0.5 * both - factor_ref[0] * grad).astype(jnp.bfloat16)


def block_rows(count, width):
    size = 128
    while size * 2 * width <= 1600 << 10 and size < 1024 and count % (size * 2) == 0:
        size *= 2
    return size


def finish(own, other, lefts, rights, factor, start, stop, into=None):
    depth, width = rights[0].shape
    size = block_rows(stop - start, width)
    first = start // size
    tile = pl.BlockSpec((size, width), lambda i: (first + i, 0))
    left = pl.BlockSpec((depth, size), lambda i: (0, first + i))
    right = pl.BlockSpec((depth, width), lambda i: (0, 0), pipeline_mode=pl.Buffered(1))
    operands = [factor.reshape(1), own, other, *lefts, *rights]
    specs = [pl.BlockSpec(memory_space=pltpu.SMEM), tile, tile, left, left, right, right]
    aliases = {}
    if into is not None:
        aliases = {len(operands): 0}
        operands.append(into)
        specs.append(pl.BlockSpec(memory_space=pl.ANY))
    return pl.pallas_call(
        finish_kernel,
        grid=((stop - start) // size,),
        in_specs=specs,
        out_specs=tile,
        out_shape=jax.ShapeDtypeStruct(own.shape, jnp.bfloat16),
        input_output_aliases=aliases,
        compiler_params=pltpu.CompilerParams(vmem_limit_bytes=48 << 20),
        cost_estimate=pl.CostEstimate(
            flops=4 * depth * width * (stop - start),
            bytes_accessed=6 * width * (stop - start),
            transcendentals=0,
        ),
        name="finish",
    )(*operands)


def gather_both(tok, cot):
    if not short_ring():
        slots = [[lax.all_gather(shard, "tp", axis=0, tiled=True)] for shard in (tok, cot)]
        return (*slots, (tok, cot))
    inner = flip_size()
    ring = lax.axis_size("tp") // inner
    current = [tok, cot]
    straight, flipped = [[], []], [[], []]
    for step in range(ring):
        for n in range(2):
            if step:
                held = current[n]
                if step > 1 and inner == 2:
                    held = after(held, flipped[n][step - 2])
                current[n] = step_up(held)
            straight[n].append(current[n])
        for n in range(2):
            if inner == 2:
                held = after(current[n], flipped[n][-1]) if flipped[n] else current[n]
                flipped[n].append(flip(held))
    last = tuple(f[-1] for f in flipped) if inner == 2 else tuple(current)
    return straight[0] + flipped[0], straight[1] + flipped[1], last


def near(tok, cot, w_in, w_out, rate, scale_in, scale_out, bit):
    rows = tok.shape[0]
    other_in = from_partner(w_in, bit)
    tok_slots, up_slots, last = gather_both(tok, cot)
    other_out = from_partner(after(w_out, *last), bit)
    hidden, dpre, partials, tokens, upstream = forward(
        tok_slots, up_slots, w_in, w_out, scale_in, scale_out
    )
    other_tok = from_partner(tokens, bit)
    other_up = from_partner(upstream, bit)
    other_hidden = from_partner(hidden, bit)
    other_dpre = from_partner(dpre, bit)
    factor_in, factor_out = 0.5 * rate * scale_in, 0.5 * rate * scale_out
    sides = [
        (w_in, other_in, (tokens, other_tok), (dpre, other_dpre), factor_in),
        (w_out, other_out, (hidden, other_hidden), (upstream, other_up), factor_out),
    ]

    def piece(side, start, stop, continues):
        def run(gate, given):
            own, other, lefts, rights, factor = sides[side]
            factor = after(factor, gate)
            if continues:
                return (*given[:-1], finish(own, other, lefts, rights, factor, start, stop, given[-1]))
            return (*given, finish(own, other, lefts, rights, factor, start, stop))

        return run

    pieces = []
    for side in range(2):
        count = sides[side][0].shape[0]
        half = count // 256 * 128
        pieces += [piece(side, 0, half, False), piece(side, half, count, True)]
    input_grad, (mixed_in, mixed_out) = scatter_sum(partials, rows, pieces)
    return input_grad, mixed_in, mixed_out


def update_kernel(factor_ref, own_ref, left_ref, right_ref, *out_refs, cuts):
    for out_ref, (lo, hi) in zip(out_refs, cuts):
        grad = dot_tn(left_ref[...], right_ref[:, lo:hi])
        out_ref[...] = (own_ref[:, lo:hi].astype(jnp.float32) - factor_ref[0] * grad).astype(jnp.bfloat16)


def update(own, left, right, factor, cuts):
    depth, width = right.shape
    count = own.shape[0]
    size = block_rows(count, width)
    return pl.pallas_call(
        partial(update_kernel, cuts=cuts),
        grid=(count // size,),
        in_specs=[
            pl.BlockSpec(memory_space=pltpu.SMEM),
            pl.BlockSpec((size, width), lambda i: (i, 0)),
            pl.BlockSpec((depth, size), lambda i: (0, i)),
            pl.BlockSpec((depth, width), lambda i: (0, 0), pipeline_mode=pl.Buffered(1)),
        ],
        out_specs=[pl.BlockSpec((size, hi - lo), lambda i: (i, 0)) for lo, hi in cuts],
        out_shape=[jax.ShapeDtypeStruct((count, hi - lo), jnp.bfloat16) for lo, hi in cuts],
        compiler_params=pltpu.CompilerParams(vmem_limit_bytes=48 << 20),
        cost_estimate=pl.CostEstimate(
            flops=2 * depth * width * count, bytes_accessed=4 * width * count, transcendentals=0
        ),
        name="update",
    )(factor.reshape(1), own, left, right)


def far(tok, cot, w_in, w_out, rate, scale_in, scale_out, bit):
    rows = tok.shape[0]
    unit = 128
    units = w_out.shape[0] // unit
    tok_other = from_partner(tok, bit)
    other_in = from_partner(w_in, bit)
    sent = [tok_other, other_in]

    def send(value):
        sent.append(from_partner(after(value, sent[-2]), bit))
        return sent[-1]

    tok_slots, up_slots, _ = gather_both(tok, cot)
    hidden, dpre, partials, tokens, upstream = forward(
        tok_slots, up_slots, w_in, w_out, scale_in, scale_out
    )
    dpre_other = from_partner(after(dpre, tok_other), bit)
    (new_out,) = update(w_out, hidden, upstream, rate * scale_out, ((0, w_out.shape[1]),))
    input_grad, _ = scatter_sum(after(partials, new_out), rows)
    tokens_other = gather_rows(after(tok_other, input_grad))[0]
    marks = [0, units // 4, units // 2, 3 * units // 4, units - 1, units]
    cuts = [(lo * unit, hi * unit) for lo, hi in zip(marks, marks[1:]) if lo < hi]
    mixed_in, mixed_out = None, jnp.zeros_like(w_out)
    for number, (lo, hi) in enumerate(cuts):
        own = new_out[lo:hi]
        other = send(own)
        mixed_out = lax.dynamic_update_slice(mixed_out, mean_of(own, other), (lo, 0))
        if number == 0:
            factor = after(0.5 * rate * scale_in, other)
            mixed_in = finish(
                w_in, other_in, (tokens, tokens_other), (dpre, dpre_other), factor, 0, w_in.shape[0]
            )
    return input_grad, mixed_in, mixed_out


def per_device(tokens, cotangent, w_in, w_out, gossip_step):
    width = tokens.shape[2]
    hid_dev = w_in.shape[2]
    scale_in = 1.0 / width**0.5
    scale_out = 1.0 / (hid_dev * lax.axis_size("tp")) ** 0.5
    rate = 16.0 / (8.0 + gossip_step[0].astype(jnp.float32))
    nbits = lax.axis_size("rep").bit_length() - 1
    branches = [
        partial(near if bit == 0 else far, scale_in=scale_in, scale_out=scale_out, bit=bit)
        for bit in range(nbits)
    ]
    input_grad, mixed_in, mixed_out = lax.switch(
        gossip_step[0] % nbits, branches, tokens[0], cotangent[0], w_in[0], w_out[0], rate
    )
    return (input_grad[None], mixed_in[None], mixed_out[None])


def solution(mesh):
    return jax.shard_map(
        per_device,
        mesh=mesh,
        in_specs=(
            P("rep", "tp", None),
            P("rep", "tp", None),
            P("rep", None, "tp"),
            P("rep", "tp", None),
            P(),
        ),
        out_specs=(P("rep", "tp", None), P("rep", None, "tp"), P("rep", "tp", None)),
        check_vma=False,
    )
```

profile of v0, /device:TPU:0, one launch (start us, length us, event | category | flops | bytes accessed | tf_op | source)
XLA Modules:
  0.0 164.0 jit_solution(4283424544121985432)
XLA Ops:
  1.3 162.0 %conditional.1 = (bf16[6144,1536]{1,0:T(8,128)(2,1)}, bf16[1536,6144]{1,0:T(8,128)(2,1)}, bf16[1,24,6144]{2,1,0:T(8,128)(2,1)S(1)}) conditional(s32[]{:T(128)} %clamp.3, (bf16[24,6144]{1,0:T(8,128)(2,1)}, bf16[24,6144]{1,0:T(8,128)(2,1)}, bf16[6144,1536]{1,0:T(8,128)(2,1)}, bf16[1536,6144]{1,0:T(8,128)(2,1)}, f32[]{:T(128)}) %tuple.67, (f32[]{:T(128)}, ...), branch_computations={%region_0.1_spmd, %region_1.2_spmd} | conditional | flops 25370394624 | bytes 567117184 | solution.py:374
  1.9 2.6 %collective-permute-start = (bf16[24,6144]{1,0:T(8,128)(2,1)}, bf16[24,6144]{1,0:T(8,128)(2,1)S(1)}, u32[]{:S(2)}, u32[]{:S(2)}) collective-permute-start(bf16[24,6144]{1,0:T(8,128)(2,1)} %get-tuple-element.21.refs_0_), channel_id=1, source_target_pairs={{0,2},{1,3},{2,4},{3,5},{4,6},{5,7},{6,0},{7,1},{8,10},{9,11},{10,... | collective-permute-start | bytes 884744 | tf_op jit(solution)/shard_map/cond/branch_0_fun/ppermute | solution.py:33
  4.5 1.5 collective-permute-start.1
  6.0 1.6 collective-permute-start.7
  8.1 6.5 %collective-permute-done.refs_1_ = bf16[24,6144]{1,0:T(8,128)(2,1)S(1)} collective-permute-done((bf16[24,6144]{1,0:T(8,128)(2,1)}, bf16[24,6144]{1,0:T(8,128)(2,1)S(1)}, u32[]{:S(2)}, u32[]{:S(2)}) %collective-permute-start) | collective-permute-done | bytes 294944 | tf_op jit(solution)/shard_map/cond/branch_0_fun/ppermute | solution.py:33
  14.6 1.5 collective-permute-start.2
  16.1 1.5 collective-permute-start.3
  17.6 3.3 %collective-permute-done.7.refs_9_ = bf16[24,6144]{1,0:T(8,128)(2,1)S(1)} collective-permute-done((bf16[24,6144]{1,0:T(8,128)(2,1)}, bf16[24,6144]{1,0:T(8,128)(2,1)S(1)}, u32[]{:S(2)}, u32[]{:S(2)}) %collective-permute-start.7) | collective-permute-done | bytes 294944 | tf_op jit(solution)/shard_map/cond/branch_0_fun/ppermute | solution.py:33
  20.9 1.5 collective-permute-start.9
  22.5 1.5 collective-permute-start.10
  24.0 3.3 %collective-permute-done.2.refs_2_ = bf16[24,6144]{1,0:T(8,128)(2,1)S(1)} collective-permute-done((bf16[24,6144]{1,0:T(8,128)(2,1)S(1)}, bf16[24,6144]{1,0:T(8,128)(2,1)S(1)}, u32[]{:S(2)}, u32[]{:S(2)}) %collective-permute-start.2) | collective-permute-done | bytes 294944 | tf_op jit(solution)/shard_map/cond/branch_0_fun/ppermute | solution.py:33
  27.2 1.5 collective-permute-start.4
  28.8 1.5 collective-permute-start.5
  30.3 3.3 %collective-permute-done.9.refs_10_ = bf16[24,6144]{1,0:T(8,128)(2,1)S(1)} collective-permute-done((bf16[24,6144]{1,0:T(8,128)(2,1)S(1)}, bf16[24,6144]{1,0:T(8,128)(2,1)S(1)}, u32[]{:S(2)}, u32[]{:S(2)}) %collective-permute-start.9) | collective-permute-done | bytes 294944 | tf_op jit(solution)/shard_map/cond/branch_0_fun/ppermute | solution.py:33
  33.6 1.5 collective-permute-start.11
  35.1 1.5 collective-permute-start.12
  36.6 3.3 %collective-permute-done.4.refs_3_ = bf16[24,6144]{1,0:T(8,128)(2,1)S(1)} collective-permute-done((bf16[24,6144]{1,0:T(8,128)(2,1)S(1)}, bf16[24,6144]{1,0:T(8,128)(2,1)S(1)}, u32[]{:S(2)}, u32[]{:S(2)}) %collective-permute-start.4) | collective-permute-done | bytes 294944 | tf_op jit(solution)/shard_map/cond/branch_0_fun/ppermute | solution.py:33
  39.9 1.6 collective-permute-start.6
  41.5 4.4 %collective-permute-done.11.refs_11_ = bf16[24,6144]{1,0:T(8,128)(2,1)S(1)} collective-permute-done((bf16[24,6144]{1,0:T(8,128)(2,1)S(1)}, bf16[24,6144]{1,0:T(8,128)(2,1)S(1)}, u32[]{:S(2)}, u32[]{:S(2)}) %collective-permute-start.11) | collective-permute-done | bytes 294944 | tf_op jit(solution)/shard_map/cond/branch_0_fun/ppermute | solution.py:33
  46.2 1.5 collective-permute-start.13
  47.7 4.8 %collective-permute-done.6.refs_7_ = bf16[24,6144]{1,0:T(8,128)(2,1)S(1)} collective-permute-done((bf16[24,6144]{1,0:T(8,128)(2,1)S(1)}, bf16[24,6144]{1,0:T(8,128)(2,1)S(1)}, u32[]{:S(2)}, u32[]{:S(2)}) %collective-permute-start.6) | collective-permute-done | bytes 294944 | tf_op jit(solution)/shard_map/cond/branch_0_fun/ppermute | solution.py:37
  52.5 5.5 %collective-permute-done.13.refs_15_ = bf16[24,6144]{1,0:T(8,128)(2,1)S(1)} collective-permute-done((bf16[24,6144]{1,0:T(8,128)(2,1)S(1)}, bf16[24,6144]{1,0:T(8,128)(2,1)S(1)}, u32[]{:S(2)}, u32[]{:S(2)}) %collective-permute-start.13) | collective-permute-done | bytes 294944 | tf_op jit(solution)/shard_map/cond/branch_0_fun/ppermute | solution.py:37
  58.7 28.9 %forward.2 = (bf16[192,1536]{1,0:T(8,128)(2,1)}, bf16[192,1536]{1,0:T(8,128)(2,1)}, bf16[192,6144]{1,0:T(8,128)(2,1)}, bf16[192,6144]{1,0:T(8,128)(2,1)}, bf16[192,6144]{1,0:T(8,128)(2,1)}) custom-call(bf16[24,6144]{1,0:T(8,128)(2,1)} %get-tuple-element.21.refs_0_, bf16[24,6144]{1,0:T(8,128)(2,1)S(1)} %collective-permute-done.refs_1_, ...), custom_call_target="tpu_custom_call" | custom-call | flops 10871635968 | bytes 37748736 | tf_op jit(solution)/shard_map/cond/branch_0_fun/forward/pallas_call | solution.py:175
  89.6 1.6 collective-permute-start.16
  91.1 2.2 %collective-permute-done.19.right2_ref = bf16[192,1536]{1,0:T(8,128)(2,1)S(1)} collective-permute-done((bf16[192,1536]{1,0:T(8,128)(2,1)}, bf16[192,1536]{1,0:T(8,128)(2,1)S(1)}, u32[]{:S(2)}, u32[]{:S(2)}) %collective-permute-start.19) | collective-permute-done | bytes 589856 | tf_op jit(solution)/shard_map/cond/branch_0_fun/ppermute | solution.py:14
  95.4 1.7 %copy-done.1 = bf16[192,6144]{1,0:T(8,128)(2,1)S(1)} copy-done((bf16[192,6144]{1,0:T(8,128)(2,1)S(1)}, bf16[192,6144]{1,0:T(8,128)(2,1)}, u32[]{:S(2)}) %copy-start.1) | copy-done | bytes 2359320 | tf_op jit(solution)/shard_map/cond
  98.1 14.7 %finish.5.out_refs_0_ = bf16[6144,1536]{1,0:T(8,128)(2,1)} custom-call(f32[1]{0:T(128)} %bitcast.factor_ref, bf16[6144,1536]{1,0:T(8,128)(2,1)} %get-tuple-element.29.refs_16_.own_ref, bf16[6144,1536]{1,0:T(8,128)(2,1)} %collective-permute-done.17.other_ref, bf16[192,6144]{1,0:T(8,128)(2,1)S(1)} %copy-done.1, ...), custom_call_target="tpu_custom_call" | custom-call | flops 3623878656 | bytes 28311552 | tf_op jit(solution)/shard_map/cond/branch_0_fun/finish/pallas_call | solution.py:221
  112.8 1.6 collective-permute-start.20
  114.5 14.7 %finish.6 = bf16[6144,1536]{1,0:T(8,128)(2,1)} custom-call(f32[1]{0:T(128)} %bitcast.1.factor_ref, bf16[6144,1536]{1,0:T(8,128)(2,1)} %get-tuple-element.29.refs_16_.own_ref, bf16[6144,1536]{1,0:T(8,128)(2,1)} %collective-permute-done.17.other_ref, bf16[192,6144]{1,0:T(8,128)(2,1)S(1)} %copy-done.1, ...), custom_call_target="tpu_custom_call", output_to_operand_aliasing={{}: (7, {})} | custom-call | flops 3623878656 | bytes 28311552 | tf_op jit(solution)/shard_map/cond/branch_0_fun/finish/pallas_call | solution.py:221
  131.3 1.8 %collective-permute-start.21 = (bf16[24,6144]{1,0:T(8,128)(2,1)S(1)}, bf16[24,6144]{1,0:T(8,128)(2,1)S(1)}, u32[]{:S(2)}, u32[]{:S(2)}) collective-permute-start(bf16[24,6144]{1,0:T(8,128)(2,1)S(1)} %add_convert_fusion.2), channel_id=1, source_target_pairs={{0,2},{1,3},{2,4},{3,5},{4,6},{5,7},{6,0},{7,1},{8,10},{9,11},{10,... | collective-permute-start | bytes 884744 | tf_op jit(solution)/shard_map/cond/branch_0_fun/ppermute | solution.py:33
  133.1 14.5 %finish.7.out_refs_0_ = bf16[1536,6144]{1,0:T(8,128)(2,1)} custom-call(f32[1]{0:T(128)} %bitcast.2.factor_ref, bf16[1536,6144]{1,0:T(8,128)(2,1)} %get-tuple-element.42.refs_17_.own_ref, bf16[1536,6144]{1,0:T(8,128)(2,1)} %collective-permute-done.22.other_ref, bf16[192,1536]{1,0:T(8,128)(2,1)S(1)} %copy-done.4, ...), custom_call_target="tpu_custom_call" | custom-call | flops 3623878656 | bytes 28311552 | tf_op jit(solution)/shard_map/cond/branch_0_fun/finish/pallas_call | solution.py:221
  148.1 14.5 %finish.8 = bf16[1536,6144]{1,0:T(8,128)(2,1)} custom-call(f32[1]{0:T(128)} %bitcast.3.factor_ref, bf16[1536,6144]{1,0:T(8,128)(2,1)} %get-tuple-element.42.refs_17_.own_ref, bf16[1536,6144]{1,0:T(8,128)(2,1)} %collective-permute-done.22.other_ref, bf16[192,1536]{1,0:T(8,128)(2,1)S(1)} %copy-done.4, ...), custom_call_target="tpu_custom_call", output_to_operand_aliasing={{}: (7, {})} | custom-call | flops 3623878656 | bytes 28311552 | tf_op jit(solution)/shard_map/cond/branch_0_fun/finish/pallas_call | solution.py:221
  (61 shorter events, 10.4 us)
Async XLA Ops:
  1.3 93.5 %collective-permute-start.17 = (bf16[6144,1536]{1,0:T(8,128)(2,1)}, bf16[6144,1536]{1,0:T(8,128)(2,1)}, u32[]{:S(2)}, u32[]{:S(2)}) collective-permute-start(bf16[6144,1536]{1,0:T(8,128)(2,1)} %get-tuple-element.29.refs_16_.own_ref), channel_id=1, source_target_pairs={{0,8},{8,0},{16,24},{24,16},{1,9},{9,1},{17,25},{25,17},{2,10},{10... | collective-permute-start | bytes 56623112 | tf_op jit(solution)/shard_map/cond/branch_0_fun/ppermute | solution.py:14
  1.9 12.7 %collective-permute-start = (bf16[24,6144]{1,0:T(8,128)(2,1)}, bf16[24,6144]{1,0:T(8,128)(2,1)S(1)}, u32[]{:S(2)}, u32[]{:S(2)}) collective-permute-start(bf16[24,6144]{1,0:T(8,128)(2,1)} %get-tuple-element.21.refs_0_), channel_id=1, source_target_pairs={{0,2},{1,3},{2,4},{3,5},{4,6},{5,7},{6,0},{7,1},{8,10},{9,11},{10,... | collective-permute-start | bytes 884744 | tf_op jit(solution)/shard_map/cond/branch_0_fun/ppermute | solution.py:33
  4.5 10.1 %collective-permute-start.1 = (bf16[24,6144]{1,0:T(8,128)(2,1)}, bf16[24,6144]{1,0:T(8,128)(2,1)S(1)}, u32[]{:S(2)}, u32[]{:S(2)}) collective-permute-start(bf16[24,6144]{1,0:T(8,128)(2,1)} %get-tuple-element.21.refs_0_), channel_id=1, source_target_pairs={{0,1},{1,0},{2,3},{3,2},{4,5},{5,4},{6,7},{7,6},{8,9},{9,8},{10,11... | collective-permute-start | bytes 884744 | tf_op jit(solution)/shard_map/cond/branch_0_fun/ppermute | solution.py:37
  6.0 14.9 %collective-permute-start.7 = (bf16[24,6144]{1,0:T(8,128)(2,1)}, bf16[24,6144]{1,0:T(8,128)(2,1)S(1)}, u32[]{:S(2)}, u32[]{:S(2)}) collective-permute-start(bf16[24,6144]{1,0:T(8,128)(2,1)} %get-tuple-element.25.refs_8_), channel_id=1, source_target_pairs={{0,2},{1,3},{2,4},{3,5},{4,6},{5,7},{6,0},{7,1},{8,10},{9,11},{10,... | collective-permute-start | bytes 884744 | tf_op jit(solution)/shard_map/cond/branch_0_fun/ppermute | solution.py:33
  7.6 13.4 %collective-permute-start.8 = (bf16[24,6144]{1,0:T(8,128)(2,1)}, bf16[24,6144]{1,0:T(8,128)(2,1)S(1)}, u32[]{:S(2)}, u32[]{:S(2)}) collective-permute-start(bf16[24,6144]{1,0:T(8,128)(2,1)} %get-tuple-element.25.refs_8_), channel_id=1, source_target_pairs={{0,1},{1,0},{2,3},{3,2},{4,5},{5,4},{6,7},{7,6},{8,9},{9,8},{10,11... | collective-permute-start | bytes 884744 | tf_op jit(solution)/shard_map/cond/branch_0_fun/ppermute | solution.py:37
  14.6 12.6 %collective-permute-start.2 = (bf16[24,6144]{1,0:T(8,128)(2,1)S(1)}, bf16[24,6144]{1,0:T(8,128)(2,1)S(1)}, u32[]{:S(2)}, u32[]{:S(2)}) collective-permute-start(bf16[24,6144]{1,0:T(8,128)(2,1)S(1)} %collective-permute-done.refs_1_), channel_id=1, source_target_pairs={{0,2},{1,3},{2,4},{3,5},{4,6},{5,7},{6,0},{7,1},{8,10},{9,11},{10,... | collective-permute-start | bytes 884744 | tf_op jit(solution)/shard_map/cond/branch_0_fun/ppermute | solution.py:33
  16.1 11.1 %collective-permute-start.3 = (bf16[24,6144]{1,0:T(8,128)(2,1)S(1)}, bf16[24,6144]{1,0:T(8,128)(2,1)S(1)}, u32[]{:S(2)}, u32[]{:S(2)}) collective-permute-start(bf16[24,6144]{1,0:T(8,128)(2,1)S(1)} %collective-permute-done.refs_1_), channel_id=1, source_target_pairs={{0,1},{1,0},{2,3},{3,2},{4,5},{5,4},{6,7},{7,6},{8,9},{9,8},{10,11... | collective-permute-start | bytes 884744 | tf_op jit(solution)/shard_map/cond/branch_0_fun/ppermute | solution.py:37
  20.9 37.1 %copy-start.14 = (bf16[24,6144]{1,0:T(8,128)(2,1)}, bf16[24,6144]{1,0:T(8,128)(2,1)S(1)}, u32[]{:S(2)}) copy-start(bf16[24,6144]{1,0:T(8,128)(2,1)S(1)} %collective-permute-done.7.refs_9_) | copy-start | bytes 884740 | tf_op jit(solution)/shard_map/cond
  20.9 37.1 %copy-start.16 = (bf16[24,6144]{1,0:T(8,128)(2,1)}, bf16[24,6144]{1,0:T(8,128)(2,1)S(1)}, u32[]{:S(2)}) copy-start(bf16[24,6144]{1,0:T(8,128)(2,1)S(1)} %collective-permute-done.8.refs_12_) | copy-start | bytes 884740 | tf_op jit(solution)/shard_map/cond
  20.9 12.6 %collective-permute-start.9 = (bf16[24,6144]{1,0:T(8,128)(2,1)S(1)}, bf16[24,6144]{1,0:T(8,128)(2,1)S(1)}, u32[]{:S(2)}, u32[]{:S(2)}) collective-permute-start(bf16[24,6144]{1,0:T(8,128)(2,1)S(1)} %collective-permute-done.7.refs_9_), channel_id=1, source_target_pairs={{0,2},{1,3},{2,4},{3,5},{4,6},{5,7},{6,0},{7,1},{8,10},{9,11},{10,... | collective-permute-start | bytes 884744 | tf_op jit(solution)/shard_map/cond/branch_0_fun/ppermute | solution.py:33
  22.5 11.1 %collective-permute-start.10 = (bf16[24,6144]{1,0:T(8,128)(2,1)S(1)}, bf16[24,6144]{1,0:T(8,128)(2,1)S(1)}, u32[]{:S(2)}, u32[]{:S(2)}) collective-permute-start(bf16[24,6144]{1,0:T(8,128)(2,1)S(1)} %collective-permute-done.7.refs_9_), channel_id=1, source_target_pairs={{0,1},{1,0},{2,3},{3,2},{4,5},{5,4},{6,7},{7,6},{8,9},{9,8},{10,11... | collective-permute-start | bytes 884744 | tf_op jit(solution)/shard_map/cond/branch_0_fun/ppermute | solution.py:37
  27.2 12.6 %collective-permute-start.4 = (bf16[24,6144]{1,0:T(8,128)(2,1)S(1)}, bf16[24,6144]{1,0:T(8,128)(2,1)S(1)}, u32[]{:S(2)}, u32[]{:S(2)}) collective-permute-start(bf16[24,6144]{1,0:T(8,128)(2,1)S(1)} %collective-permute-done.2.refs_2_), channel_id=1, source_target_pairs={{0,2},{1,3},{2,4},{3,5},{4,6},{5,7},{6,0},{7,1},{8,10},{9,11},{10,... | collective-permute-start | bytes 884744 | tf_op jit(solution)/shard_map/cond/branch_0_fun/ppermute | solution.py:33
  28.8 11.1 %collective-permute-start.5 = (bf16[24,6144]{1,0:T(8,128)(2,1)S(1)}, bf16[24,6144]{1,0:T(8,128)(2,1)S(1)}, u32[]{:S(2)}, u32[]{:S(2)}) collective-permute-start(bf16[24,6144]{1,0:T(8,128)(2,1)S(1)} %collective-permute-done.2.refs_2_), channel_id=1, source_target_pairs={{0,1},{1,0},{2,3},{3,2},{4,5},{5,4},{6,7},{7,6},{8,9},{9,8},{10,11... | collective-permute-start | bytes 884744 | tf_op jit(solution)/shard_map/cond/branch_0_fun/ppermute | solution.py:37
  33.6 24.5 %copy-start.18 = (bf16[24,6144]{1,0:T(8,128)(2,1)}, bf16[24,6144]{1,0:T(8,128)(2,1)S(1)}, u32[]{:S(2)}) copy-start(bf16[24,6144]{1,0:T(8,128)(2,1)S(1)} %collective-permute-done.9.refs_10_) | copy-start | bytes 884740 | tf_op jit(solution)/shard_map/cond
  33.6 24.5 %copy-start.20 = (bf16[24,6144]{1,0:T(8,128)(2,1)}, bf16[24,6144]{1,0:T(8,128)(2,1)S(1)}, u32[]{:S(2)}) copy-start(bf16[24,6144]{1,0:T(8,128)(2,1)S(1)} %collective-permute-done.10.refs_13_) | copy-start | bytes 884740 | tf_op jit(solution)/shard_map/cond
  33.6 12.4 %collective-permute-start.11 = (bf16[24,6144]{1,0:T(8,128)(2,1)S(1)}, bf16[24,6144]{1,0:T(8,128)(2,1)S(1)}, u32[]{:S(2)}, u32[]{:S(2)}) collective-permute-start(bf16[24,6144]{1,0:T(8,128)(2,1)S(1)} %collective-permute-done.9.refs_10_), channel_id=1, source_target_pairs={{0,2},{1,3},{2,4},{3,5},{4,6},{5,7},{6,0},{7,1},{8,10},{9,11},{10,... | collective-permute-start | bytes 884744 | tf_op jit(solution)/shard_map/cond/branch_0_fun/ppermute | solution.py:33
  35.1 11.1 %collective-permute-start.12 = (bf16[24,6144]{1,0:T(8,128)(2,1)S(1)}, bf16[24,6144]{1,0:T(8,128)(2,1)S(1)}, u32[]{:S(2)}, u32[]{:S(2)}) collective-permute-start(bf16[24,6144]{1,0:T(8,128)(2,1)S(1)} %collective-permute-done.9.refs_10_), channel_id=1, source_target_pairs={{0,1},{1,0},{2,3},{3,2},{4,5},{5,4},{6,7},{7,6},{8,9},{9,8},{10,11... | collective-permute-start | bytes 884744 | tf_op jit(solution)/shard_map/cond/branch_0_fun/ppermute | solution.py:37
  39.9 12.6 %collective-permute-start.6 = (bf16[24,6144]{1,0:T(8,128)(2,1)S(1)}, bf16[24,6144]{1,0:T(8,128)(2,1)S(1)}, u32[]{:S(2)}, u32[]{:S(2)}) collective-permute-start(bf16[24,6144]{1,0:T(8,128)(2,1)S(1)} %collective-permute-done.4.refs_3_), channel_id=1, source_target_pairs={{0,1},{1,0},{2,3},{3,2},{4,5},{5,4},{6,7},{7,6},{8,9},{9,8},{10,11... | collective-permute-start | bytes 884744 | tf_op jit(solution)/shard_map/cond/branch_0_fun/ppermute | solution.py:37
  46.2 11.9 %collective-permute-start.13 = (bf16[24,6144]{1,0:T(8,128)(2,1)S(1)}, bf16[24,6144]{1,0:T(8,128)(2,1)S(1)}, u32[]{:S(2)}, u32[]{:S(2)}) collective-permute-start(bf16[24,6144]{1,0:T(8,128)(2,1)S(1)} %collective-permute-done.11.refs_11_), channel_id=1, source_target_pairs={{0,1},{1,0},{2,3},{3,2},{4,5},{5,4},{6,7},{7,6},{8,9},{9,8},{10,11... | collective-permute-start | bytes 884744 | tf_op jit(solution)/shard_map/cond/branch_0_fun/ppermute | solution.py:37
  58.0 75.1 %collective-permute-start.22 = (bf16[1536,6144]{1,0:T(8,128)(2,1)}, bf16[1536,6144]{1,0:T(8,128)(2,1)}, u32[]{:S(2)}, u32[]{:S(2)}) collective-permute-start(bf16[1536,6144]{1,0:T(8,128)(2,1)} %get-tuple-element.42.refs_17_.own_ref), channel_id=1, source_target_pairs={{0,8},{8,0},{16,24},{24,16},{1,9},{9,1},{17,25},{25,17},{2,10},{10... | collective-permute-start | bytes 56623112 | tf_op jit(solution)/shard_map/cond/branch_0_fun/ppermute | solution.py:14
  87.7 7.1 %collective-permute-start.18 = (bf16[192,6144]{1,0:T(8,128)(2,1)}, bf16[192,6144]{1,0:T(8,128)(2,1)S(1)}, u32[]{:S(2)}, u32[]{:S(2)}) collective-permute-start(bf16[192,6144]{1,0:T(8,128)(2,1)} %get-tuple-element.34.left_ref), channel_id=1, source_target_pairs={{0,8},{8,0},{16,24},{24,16},{1,9},{9,1},{17,25},{25,17},{2,10},{10... | collective-permute-start | bytes 7077896 | tf_op jit(solution)/shard_map/cond/branch_0_fun/ppermute | solution.py:14
  87.8 5.6 %collective-permute-start.19 = (bf16[192,1536]{1,0:T(8,128)(2,1)}, bf16[192,1536]{1,0:T(8,128)(2,1)S(1)}, u32[]{:S(2)}, u32[]{:S(2)}) collective-permute-start(bf16[192,1536]{1,0:T(8,128)(2,1)} %get-tuple-element.35.right_ref), channel_id=1, source_target_pairs={{0,8},{8,0},{16,24},{24,16},{1,9},{9,1},{17,25},{25,17},{2,10},{10... | collective-permute-start | bytes 1769480 | tf_op jit(solution)/shard_map/cond/branch_0_fun/ppermute | solution.py:14
  89.6 23.2 %collective-permute-start.16 = (bf16[24,6144]{1,0:T(8,128)(2,1)S(1)}, bf16[24,6144]{1,0:T(8,128)(2,1)S(1)}, u32[]{:S(2)}, u32[]{:S(2)}) collective-permute-start(bf16[24,6144]{1,0:T(8,128)(2,1)S(1)} %get-tuple-element.87), channel_id=1, source_target_pairs={{0,1},{1,0},{2,3},{3,2},{4,5},{5,4},{6,7},{7,6},{8,9},{9,8},{10,11... | collective-permute-start | bytes 884744 | tf_op jit(solution)/shard_map/cond/branch_0_fun/ppermute | solution.py:37
  93.3 36.4 %collective-permute-start.15 = (bf16[24,6144]{1,0:T(8,128)(2,1)S(1)}, bf16[24,6144]{1,0:T(8,128)(2,1)S(1)}, u32[]{:S(2)}, u32[]{:S(2)}) collective-permute-start(bf16[24,6144]{1,0:T(8,128)(2,1)S(1)} %get-tuple-element.88), channel_id=1, source_target_pairs={{0,1},{1,0},{2,3},{3,2},{4,5},{5,4},{6,7},{7,6},{8,9},{9,8},{10,11... | collective-permute-start | bytes 884744 | tf_op jit(solution)/shard_map/cond/branch_0_fun/ppermute | solution.py:37
  94.8 36.5 %collective-permute-start.23 = (bf16[192,1536]{1,0:T(8,128)(2,1)}, bf16[192,1536]{1,0:T(8,128)(2,1)S(1)}, u32[]{:S(2)}, u32[]{:S(2)}) collective-permute-start(bf16[192,1536]{1,0:T(8,128)(2,1)} %get-tuple-element.43.left_ref), channel_id=1, source_target_pairs={{0,8},{8,0},{16,24},{24,16},{1,9},{9,1},{17,25},{25,17},{2,10},{10... | collective-permute-start | bytes 1769480 | tf_op jit(solution)/shard_map/cond/branch_0_fun/ppermute | solution.py:14
  94.8 38.3 %collective-permute-start.24 = (bf16[192,6144]{1,0:T(8,128)(2,1)}, bf16[192,6144]{1,0:T(8,128)(2,1)S(1)}, u32[]{:S(2)}, u32[]{:S(2)}) collective-permute-start(bf16[192,6144]{1,0:T(8,128)(2,1)} %get-tuple-element.44.right_ref), channel_id=1, source_target_pairs={{0,8},{8,0},{16,24},{24,16},{1,9},{9,1},{17,25},{25,17},{2,10},{10... | collective-permute-start | bytes 7077896 | tf_op jit(solution)/shard_map/cond/branch_0_fun/ppermute | solution.py:14
  112.8 16.3 %collective-permute-start.20 = (bf16[24,6144]{1,0:T(8,128)(2,1)S(1)}, bf16[24,6144]{1,0:T(8,128)(2,1)S(1)}, u32[]{:S(2)}, u32[]{:S(2)}) collective-permute-start(bf16[24,6144]{1,0:T(8,128)(2,1)S(1)} %add_convert_fusion.3), channel_id=1, source_target_pairs={{0,2},{1,3},{2,4},{3,5},{4,6},{5,7},{6,0},{7,1},{8,10},{9,11},{10,... | collective-permute-start | bytes 884744 | tf_op jit(solution)/shard_map/cond/branch_0_fun/ppermute | solution.py:33
  114.5 18.7 %copy-start.4 = (bf16[192,1536]{1,0:T(8,128)(2,1)S(1)}, bf16[192,1536]{1,0:T(8,128)(2,1)}, u32[]{:S(2)}) copy-start(bf16[192,1536]{1,0:T(8,128)(2,1)} %get-tuple-element.43.left_ref) | copy-start | bytes 1769476 | tf_op jit(solution)/shard_map/cond
  129.2 18.5 %collective-permute-start.14 = (bf16[24,6144]{1,0:T(8,128)(2,1)S(1)}, bf16[24,6144]{1,0:T(8,128)(2,1)S(1)}, u32[]{:S(2)}, u32[]{:S(2)}) collective-permute-start(bf16[24,6144]{1,0:T(8,128)(2,1)S(1)} %get-tuple-element.89), channel_id=1, source_target_pairs={{0,1},{1,0},{2,3},{3,2},{4,5},{5,4},{6,7},{7,6},{8,9},{9,8},{10,11... | collective-permute-start | bytes 884744 | tf_op jit(solution)/shard_map/cond/branch_0_fun/ppermute | solution.py:37
  129.7 33.0 %collective-permute-start.26 = (bf16[24,6144]{1,0:T(8,128)(2,1)S(1)}, bf16[24,6144]{1,0:T(8,128)(2,1)S(1)}, u32[]{:S(2)}, u32[]{:S(2)}) collective-permute-start(bf16[24,6144]{1,0:T(8,128)(2,1)S(1)} %get-tuple-element.86), channel_id=1, source_target_pairs={{0,1},{1,0},{2,3},{3,2},{4,5},{5,4},{6,7},{7,6},{8,9},{9,8},{10,11... | collective-permute-start | bytes 884744 | tf_op jit(solution)/shard_map/cond/branch_0_fun/ppermute | solution.py:37
  131.3 16.4 %collective-permute-start.21 = (bf16[24,6144]{1,0:T(8,128)(2,1)S(1)}, bf16[24,6144]{1,0:T(8,128)(2,1)S(1)}, u32[]{:S(2)}, u32[]{:S(2)}) collective-permute-start(bf16[24,6144]{1,0:T(8,128)(2,1)S(1)} %add_convert_fusion.2), channel_id=1, source_target_pairs={{0,2},{1,3},{2,4},{3,5},{4,6},{5,7},{6,0},{7,1},{8,10},{9,11},{10,... | collective-permute-start | bytes 884744 | tf_op jit(solution)/shard_map/cond/branch_0_fun/ppermute | solution.py:33
  147.8 14.9 %collective-permute-start.25 = (bf16[24,6144]{1,0:T(8,128)(2,1)S(1)}, bf16[24,6144]{1,0:T(8,128)(2,1)S(1)}, u32[]{:S(2)}, u32[]{:S(2)}) collective-permute-start(bf16[24,6144]{1,0:T(8,128)(2,1)S(1)} %add_convert_fusion.1), channel_id=1, source_target_pairs={{0,2},{1,3},{2,4},{3,5},{4,6},{5,7},{6,0},{7,1},{8,10},{9,11},{10,... | collective-permute-start | bytes 884744 | tf_op jit(solution)/shard_map/cond/branch_0_fun/ppermute | solution.py:33
  (9 other events, 67.1 us)
where the time goes:
time: 164 us
  Pallas kernels  87.3 us (53%)
  waiting for transfers between devices  36.9 us (22%)
  starting transfers between devices  31.9 us (19%)
  local copies, waits for them, and re-layouts  5.42 us (3%)
    pallas_call x4, Pallas kernels, finish(): pl.pallas_call(finish_kernel, grid=((stop - start) // size,), in_specs=sp...  58.4 us
    pallas_call x1, Pallas kernels, forward(): pl.pallas_call(partial(forward_kernel, slots=slots, scale_in=scale_in, sc...  28.9 us
    ppermute x9, waiting for transfers between devices, step_up(): lax.ppermute(value, 'tp', [(i, (i + inner) % size) for i in range(size)])  24.1 us
    ppermute x12, starting transfers between devices, flip(): lax.ppermute(value, 'tp', [(i, i ^ 1) for i in range(lax.axis_size('tp'))])  16.2 us
    ppermute x9, starting transfers between devices, step_up(): lax.ppermute(value, 'tp', [(i, (i + inner) % size) for i in range(size)])  14.1 us
    ppermute x12, waiting for transfers between devices, flip(): lax.ppermute(value, 'tp', [(i, i ^ 1) for i in range(lax.axis_size('tp'))])  10.6 us
    cond x26, local copies, waits for them, and re-layouts  3.41 us
  transfers between devices with their start and end apart: 27, of which 10 were waited for; matrix products, arithmetic and copies ran while one was open for 1% of the time, Pallas kernels for 53%

commit v1 on v0

--- a/solution.py
+++ b/solution.py
@@ -31,6 +31,11 @@
 def step_up(value):
     size, inner = lax.axis_size("tp"), flip_size()
     return lax.ppermute(value, "tp", [(i, (i + inner) % size) for i in range(size)])
+
+
+def step_down(value):
+    size, inner = lax.axis_size("tp"), flip_size()
+    return lax.ppermute(value, "tp", [(i, (i - inner) % size) for i in range(size)])
 
 
 def flip(value):
@@ -82,22 +87,25 @@
             work(partial_sums)
         return done, given
     inner = flip_size()
-    ring = lax.axis_size("tp") // inner
+    size = lax.axis_size("tp")
+    ring = size // inner
     slot = lambda number: partial_sums[number * rows : (number + 1) * rows]
-    arrived = [None] * ring
+    sums = [slot(k).astype(jnp.float32) for k in range(ring)]
     if inner == 2:
-        arrived = [flip(slot(ring + (k + 1) % ring)) for k in range(ring)]
-        (arrived[0],) = work(partial_sums, arrived[0])
-    carried = None
-    for k in range(ring):
-        total = slot((k + 1) % ring).astype(jnp.float32)
-        if arrived[k] is not None:
-            total = total + arrived[k].astype(jnp.float32)
-        if carried is not None:
-            total = total + carried.astype(jnp.float32)
-        carried = total.astype(jnp.bfloat16)
-        if k < ring - 1:
-            (carried,) = work(carried, step_up(carried))
+        (arrived,) = work(partial_sums, flip(partial_sums[ring * rows :]))
+        arrived = arrived.astype(jnp.float32).reshape(ring, rows, -1)
+        sums = [own + arrived[k] for k, own in enumerate(sums)]
+    leaving = [total.astype(jnp.bfloat16) for total in sums[1:]]
+    arrived = [
+        lax.ppermute(value, "tp", [(i, (i - k * inner) % size) for i in range(size)])
+        for k, value in enumerate(leaving, 1)
+    ]
+    total = sums[0]
+    if leaving:
+        arrived = work(leaving[0], *arrived)
+    for other in arrived:
+        total = total + other.astype(jnp.float32)
+    carried = total.astype(jnp.bfloat16)
     while pieces:
         work(carried)
     return carried, given
@@ -128,35 +136,31 @@
 
 def forward_kernel(*refs, slots, scale_in, scale_out):
     tok_slots, up_slots = refs[:slots], refs[slots : 2 * slots]
-    w_in_ref, w_out_ref, hidden_ref, dpre_ref, part_ref, tok_ref, up_ref, acc_ref = refs[2 * slots :]
+    w_in_ref, w_out_ref, both_ref, sides_out, tok_ref, up_ref, sems = refs[2 * slots :]
     step = pl.program_id(0)
+    copies = [
+        pltpu.make_async_copy(tok_ref, sides_out.at[0], sems.at[0]),
+        pltpu.make_async_copy(up_ref, sides_out.at[1], sems.at[1]),
+    ]
 
     @pl.when(step == 0)
     def _():
-        for whole, parts in ((tok_ref, tok_slots), (up_ref, up_slots)):
+        for whole, parts, copy in zip((tok_ref, up_ref), (tok_slots, up_slots), copies):
             rows = parts[0].shape[0]
             for number, part in enumerate(parts):
                 whole[number * rows : (number + 1) * rows, :] = part[...]
+            copy.start()
 
     preact = jnp.dot(tok_ref[...], w_in_ref[...], preferred_element_type=jnp.float32) * scale_in
     back = dot_nt(up_ref[...], w_out_ref[...]) * scale_out
     value, slope = gelu_parts(preact)
-    hidden_ref[...] = value.astype(jnp.bfloat16)
-    dpre = (back * slope).astype(jnp.bfloat16)
-    dpre_ref[...] = dpre
-    part = dot_nt(dpre, w_in_ref[...])
-
-    @pl.when(step == 0)
-    def _():
-        acc_ref[...] = part
-
-    @pl.when(step > 0)
-    def _():
-        acc_ref[...] += part
+    both_ref[0] = value.astype(jnp.bfloat16)
+    both_ref[1] = (back * slope).astype(jnp.bfloat16)
 
     @pl.when(step == pl.num_programs(0) - 1)
     def _():
-        part_ref[...] = (acc_ref[...] * scale_in).astype(jnp.bfloat16)
+        for copy in copies:
+            copy.wait()
 
 
 def forward(tok_slots, up_slots, w_in, w_out, scale_in, scale_out):
@@ -165,36 +169,42 @@
     rows, cols = slots * part_rows, 256
     if rows > 256 or hid % cols:
         tokens, upstream = jnp.concatenate(tok_slots, axis=0), jnp.concatenate(up_slots, axis=0)
-        hidden, dpre = activations(tokens, upstream, w_in, w_out, scale_in, scale_out)
-        partials = (dot_nt(dpre, w_in) * scale_in).astype(jnp.bfloat16)
-        return hidden, dpre, partials, tokens, upstream
-    once = lambda count: pl.BlockSpec((count, width), lambda i: (0, 0), pipeline_mode=pl.Buffered(1))
-    block = pl.BlockSpec((rows, cols), lambda i: (0, i))
-    wide = jax.ShapeDtypeStruct((rows, width), jnp.bfloat16)
-    tall = jax.ShapeDtypeStruct((rows, hid), jnp.bfloat16)
+        both = activations(tokens, upstream, w_in, w_out, scale_in, scale_out)
+        return jnp.stack(both), jnp.stack([tokens, upstream])
+    once = pl.BlockSpec((part_rows, width), lambda i: (0, 0), pipeline_mode=pl.Buffered(1))
     return pl.pallas_call(
         partial(forward_kernel, slots=slots, scale_in=scale_in, scale_out=scale_out),
         grid=(hid // cols,),
         in_specs=[
-            *[once(part_rows)] * (2 * slots),
+            *[once] * (2 * slots),
             pl.BlockSpec((width, cols), lambda i: (0, i)),
             pl.BlockSpec((cols, width), lambda i: (i, 0)),
         ],
-        out_specs=[block, block, *[once(rows)] * 3],
-        out_shape=[tall, tall, wide, wide, wide],
-        scratch_shapes=[pltpu.VMEM((rows, width), jnp.float32)],
-        compiler_params=pltpu.CompilerParams(vmem_limit_bytes=52 << 20),
+        out_specs=[
+            pl.BlockSpec((2, rows, cols), lambda i: (0, 0, i)),
+            pl.BlockSpec(memory_space=pl.ANY),
+        ],
+        out_shape=[
+            jax.ShapeDtypeStruct((2, rows, hid), jnp.bfloat16),
+            jax.ShapeDtypeStruct((2, rows, width), jnp.bfloat16),
+        ],
+        scratch_shapes=[
+            pltpu.VMEM((rows, width), jnp.bfloat16),
+            pltpu.VMEM((rows, width), jnp.bfloat16),
+            pltpu.SemaphoreType.DMA((2,)),
+        ],
+        compiler_params=pltpu.CompilerParams(vmem_limit_bytes=48 << 20),
         cost_estimate=pl.CostEstimate(
-            flops=6 * rows * width * hid, bytes_accessed=4 * width * hid, transcendentals=2 * rows * hid
+            flops=4 * rows * width * hid, bytes_accessed=4 * width * hid, transcendentals=2 * rows * hid
         ),
         name="forward",
     )(*tok_slots, *up_slots, w_in, w_out)
 
 
-def finish_kernel(factor_ref, own_ref, other_ref, left_ref, left2_ref, right_ref, right2_ref, *out_refs):
+def finish_kernel(factor_ref, own_ref, other_ref, left_ref, left2_ref, right_ref, right2_ref, out_ref):
     grad = dot_tn(left_ref[...], right_ref[...]) + dot_tn(left2_ref[...], right2_ref[...])
     both = own_ref[...].astype(jnp.float32) + other_ref[...].astype(jnp.float32)
-    out_refs[-1][...] = (0.5 * both - factor_ref[0] * grad).astype(jnp.bfloat16)
+    out_ref[...] = (0.5 * both - factor_ref[0] * grad).astype(jnp.bfloat16)
 
 
 def block_rows(count, width):
@@ -204,41 +214,38 @@
     return size
 
 
-def finish(own, other, lefts, rights, factor, start, stop, into=None):
-    depth, width = rights[0].shape
-    size = block_rows(stop - start, width)
-    first = start // size
-    tile = pl.BlockSpec((size, width), lambda i: (first + i, 0))
-    left = pl.BlockSpec((depth, size), lambda i: (0, first + i))
-    right = pl.BlockSpec((depth, width), lambda i: (0, 0), pipeline_mode=pl.Buffered(1))
-    operands = [factor.reshape(1), own, other, *lefts, *rights]
-    specs = [pl.BlockSpec(memory_space=pltpu.SMEM), tile, tile, left, left, right, right]
-    aliases = {}
-    if into is not None:
-        aliases = {len(operands): 0}
-        operands.append(into)
-        specs.append(pl.BlockSpec(memory_space=pl.ANY))
+def finish(own, other, lefts, rights, factor):
+    depth, width = rights[0][0].shape[1:]
+    count = own.shape[0]
+    size = block_rows(count, width)
+    tile = pl.BlockSpec((size, width), lambda i: (i, 0))
+    left = lambda place: pl.BlockSpec((None, depth, size), lambda i: (place, 0, i))
+    right = lambda place: pl.BlockSpec(
+        (None, depth, width), lambda i: (place, 0, 0), pipeline_mode=pl.Buffered(1)
+    )
     return pl.pallas_call(
         finish_kernel,
-        grid=((stop - start) // size,),
-        in_specs=specs,
+        grid=(count // size,),
+        in_specs=[
+            pl.BlockSpec(memory_space=pltpu.SMEM),
+            tile,
+            tile,
+            *[left(place) for _, place in lefts],
+            *[right(place) for _, place in rights],
+        ],
         out_specs=tile,
         out_shape=jax.ShapeDtypeStruct(own.shape, jnp.bfloat16),
-        input_output_aliases=aliases,
         compiler_params=pltpu.CompilerParams(vmem_limit_bytes=48 << 20),
         cost_estimate=pl.CostEstimate(
-            flops=4 * depth * width * (stop - start),
-            bytes_accessed=6 * width * (stop - start),
-            transcendentals=0,
+            flops=4 * depth * width * count, bytes_accessed=6 * width * count, transcendentals=0
         ),
         name="finish",
-    )(*operands)
+    )(factor.reshape(1), own, other, *[array for array, _ in lefts + rights])
 
 
 def gather_both(tok, cot):
     if not short_ring():
-        slots = [[lax.all_gather(shard, "tp", axis=0, tiled=True)] for shard in (tok, cot)]
-        return (*slots, (tok, cot))
+        return [[lax.all_gather(shard, "tp", axis=0, tiled=True)] for shard in (tok, cot)]
     inner = flip_size()
     ring = lax.axis_size("tp") // inner
     current = [tok, cot]
@@ -252,46 +259,36 @@
                 current[n] = step_up(held)
             straight[n].append(current[n])
         for n in range(2):
-            if inner == 2:
+            if inner == 2 and n == 1 and ring > 2 and step == ring - 1:
+                flipped[n].append(step_down(after(flipped[n][0], straight[n][-2])))
+            elif inner == 2:
                 held = after(current[n], flipped[n][-1]) if flipped[n] else current[n]
                 flipped[n].append(flip(held))
-    last = tuple(f[-1] for f in flipped) if inner == 2 else tuple(current)
-    return straight[0] + flipped[0], straight[1] + flipped[1], last
+    return straight[0] + flipped[0], straight[1] + flipped[1]
 
 
 def near(tok, cot, w_in, w_out, rate, scale_in, scale_out, bit):
     rows = tok.shape[0]
     other_in = from_partner(w_in, bit)
-    tok_slots, up_slots, last = gather_both(tok, cot)
-    other_out = from_partner(after(w_out, *last), bit)
-    hidden, dpre, partials, tokens, upstream = forward(
-        tok_slots, up_slots, w_in, w_out, scale_in, scale_out
-    )
-    other_tok = from_partner(tokens, bit)
-    other_up = from_partner(upstream, bit)
-    other_hidden = from_partner(hidden, bit)
-    other_dpre = from_partner(dpre, bit)
-    factor_in, factor_out = 0.5 * rate * scale_in, 0.5 * rate * scale_out
-    sides = [
-        (w_in, other_in, (tokens, other_tok), (dpre, other_dpre), factor_in),
-        (w_out, other_out, (hidden, other_hidden), (upstream, other_up), factor_out),
-    ]
-
-    def piece(side, start, stop, continues):
+    tok_slots, up_slots = gather_both(tok, cot)
+    up_slots = [after(up_slots[0], other_in), *up_slots[1:]]
+    both, sides = forward(tok_slots, up_slots, w_in, w_out, scale_in, scale_out)
+    other_both = from_partner(both, bit)
+    other_sides = from_partner(sides, bit)
+    partials = (dot_nt(both[1], w_in) * scale_in).astype(jnp.bfloat16)
+    other_out = from_partner(after(w_out, other_both, other_sides, partials), bit)
+    stacks = [
+        (w_in, other_in, ((sides, 0), (other_sides, 0)), ((both, 1), (other_both, 1)), 0.5 * rate * scale_in),
+        (w_out, other_out, ((both, 0), (other_both, 0)), ((sides, 1), (other_sides, 1)), 0.5 * rate * scale_out),
+    ]
+
+    def piece(own, other, lefts, rights, factor):
         def run(gate, given):
-            own, other, lefts, rights, factor = sides[side]
-            factor = after(factor, gate)
-            if continues:
-                return (*given[:-1], finish(own, other, lefts, rights, factor, start, stop, given[-1]))
-            return (*given, finish(own, other, lefts, rights, factor, start, stop))
+            return (*given, finish(own, other, lefts, rights, after(factor, gate)))
 
         return run
 
-    pieces = []
-    for side in range(2):
-        count = sides[side][0].shape[0]
-        half = count // 256 * 128
-        pieces += [piece(side, 0, half, False), piece(side, half, count, True)]
+    pieces = [piece(*stack) for stack in stacks]
     input_grad, (mixed_in, mixed_out) = scatter_sum(partials, rows, pieces)
     return input_grad, mixed_in, mixed_out
 
@@ -337,13 +334,13 @@
         sent.append(from_partner(after(value, sent[-2]), bit))
         return sent[-1]
 
-    tok_slots, up_slots, _ = gather_both(tok, cot)
-    hidden, dpre, partials, tokens, upstream = forward(
-        tok_slots, up_slots, w_in, w_out, scale_in, scale_out
-    )
+    tok_slots, up_slots = gather_both(tok, cot)
+    both, sides = forward(tok_slots, up_slots, w_in, w_out, scale_in, scale_out)
+    dpre = both[1]
     dpre_other = from_partner(after(dpre, tok_other), bit)
-    (new_out,) = update(w_out, hidden, upstream, rate * scale_out, ((0, w_out.shape[1]),))
-    input_grad, _ = scatter_sum(after(partials, new_out), rows)
+    (new_out,) = update(w_out, both[0], sides[1], rate * scale_out, ((0, w_out.shape[1]),))
+    partials = (dot_nt(after(dpre, new_out), w_in) * scale_in).astype(jnp.bfloat16)
+    input_grad, _ = scatter_sum(partials, rows)
     tokens_other = gather_rows(after(tok_other, input_grad))[0]
     marks = [0, units // 4, units // 2, 3 * units // 4, units - 1, units]
     cuts = [(lo * unit, hi * unit) for lo, hi in zip(marks, marks[1:]) if lo < hi]
@@ -354,9 +351,9 @@
         mixed_out = lax.dynamic_update_slice(mixed_out, mean_of(own, other), (lo, 0))
         if number == 0:
             factor = after(0.5 * rate * scale_in, other)
-            mixed_in = finish(
-                w_in, other_in, (tokens, tokens_other), (dpre, dpre_other), factor, 0, w_in.shape[0]
-            )
+            lefts = ((sides, 0), (tokens_other[None], 0))
+            rights = ((both, 1), (dpre_other[None], 0))
+            mixed_in = finish(w_in, other_in, lefts, rights, factor)
     return input_grad, mixed_in, mixed_out
 
 

time: 164 us -> 840 us (5.12)
  waiting for transfers between devices: 36.9 us -> 652 us
  other arithmetic: 0.4 us -> 29.8 us
  Pallas kernels: 87.3 us -> 58.4 us
  local copies, waits for them, and re-layouts: 5.42 us -> 32.8 us
  starting transfers between devices: 31.9 us -> 54.1 us
  matrix products: 0 us -> 10.5 us
    ppermute x6 -> x8, waiting for transfers between devices: 2.23 us -> 597 us  [from_partner(): return lax.ppermute(value, 'rep', pairs)]
    pallas_call x4 -> x2, Pallas kernels: 58.4 us -> 40.9 us  [the longest x1 24.8 us: finish(): pl.pallas_call(finish_kernel, grid=(count // size,), in_specs=[pl.BlockSp...]
    dynamic_update_slice x0 -> x3, other arithmetic: none -> 14.8 us  [far(): lax.dynamic_update_slice(mixed_out, mean_of(own, other), (lo, 0))]
    slice x1 -> x4, local copies, waits for them, and re-layouts: 1.3 us -> 15.4 us  [the longest x3 15.3 us: far(): own = new_out[lo:hi]]
    ppermute x0 -> x4, waiting for transfers between devices: none -> 11.7 us  [the longest x3 8.38 us: scatter_sum(): lax.ppermute(value, 'tp', [(i, (i - k * inner) % size) for i in range(siz...]
    pallas_call x1, Pallas kernels: 28.9 us -> 17.5 us  [forward(): pl.pallas_call(partial(forward_kernel, slots=slots, scale_in=scale_in, sc...]
    dot_general x0 -> x1, matrix products: none -> 10.5 us  [dot_nt(): lax.dot_general(left, right, (((1,), (1,)), ((), ())), preferred_element_...]
    ppermute x9, waiting for transfers between devices: 24.1 us -> 34.6 us  [step_up(): lax.ppermute(value, 'tp', [(i, (i + inner) % size) for i in range(size)])]
  transfers between devices with their start and end apart: 27 -> 33, of which waited for: 10 -> 18; matrix products, arithmetic and copies ran while one was open for 1% -> 7% of each run, Pallas kernels for 53% -> 7%
where the time goes in v1:
time: 840 us; the launch traced here: 839 us
  waiting for transfers between devices  652 us (78%)
  Pallas kernels  58.4 us (7%)
  starting transfers between devices  54.1 us (6%)
  local copies, waits for them, and re-layouts  32.8 us (4%)
  other arithmetic  29.8 us (4%)
  matrix products  10.5 us (1%)
    ppermute x8, waiting for transfers between devices, from_partner(): return lax.ppermute(value, 'rep', pairs)  597 us
    ppermute x9, waiting for transfers between devices, step_up(): lax.ppermute(value, 'tp', [(i, (i + inner) % size) for i in range(size)])  34.6 us
    pallas_call x1, Pallas kernels, finish(): pl.pallas_call(finish_kernel, grid=(count // size,), in_specs=[pl.BlockSp...  24.8 us
    ppermute x9, starting transfers between devices, step_up(): lax.ppermute(value, 'tp', [(i, (i + inner) % size) for i in range(size)])  19.7 us
    pallas_call x1, Pallas kernels, forward(): pl.pallas_call(partial(forward_kernel, slots=slots, scale_in=scale_in, sc...  17.5 us
  transfers between devices with their start and end apart: 33, of which 18 were waited for; matrix products, arithmetic and copies ran while one was open for 7% of the time, Pallas kernels for 7%

profile of v1, /device:TPU:0, one launch (start us, length us, event | category | flops | bytes accessed | tf_op | source)
XLA Modules:
  0.0 839.0 jit_solution(8275852168136611109)
XLA Ops:
  1.3 837.0 %conditional.1 = (bf16[6144,1536]{1,0:T(8,128)(2,1)}, bf16[1536,6144]{1,0:T(8,128)(2,1)}, bf16[1,24,6144]{2,1,0:T(8,128)(2,1)S(1)}) conditional(s32[]{:T(128)} %clamp.3, (bf16[24,6144]{1,0:T(8,128)(2,1)}, bf16[6144,1536]{1,0:T(8,128)(2,1)}, bf16[24,6144]{1,0:T(8,128)(2,1)}, bf16[1536,6144]{1,0:T(8,128)(2,1)}, f32[]{:T(128)}) %tuple.63, (f32[]{:T(128)}, ...), branch_computations={%region_0.1_spmd, %region_1.2_spmd} | conditional | flops 25372753920 | bytes 594052608 | solution.py:371
  1.4 3.0 collective-permute-start.38
  9.6 6.8 collective-permute-done.22.refs_1_
  19.2 3.5 collective-permute-done.29.refs_9_
  25.5 3.5 collective-permute-done.24.refs_2_
  31.8 3.5 collective-permute-done.31.refs_10_
  38.2 3.5 collective-permute-done.26.refs_3_
  49.7 3.3 collective-permute-done.35.refs_15_
  58.6 17.5 %forward.3 = (bf16[2,192,1536]{2,1,0:T(8,128)(2,1)S(1)}, bf16[2,192,6144]{2,1,0:T(8,128)(2,1)}) custom-call(bf16[24,6144]{1,0:T(8,128)(2,1)} %get-tuple-element.47.refs_0_, bf16[24,6144]{1,0:T(8,128)(2,1)S(1)} %collective-permute-done.22.refs_1_, bf16[24,6144]{1,0:T(8,128)(2,1)S(1)} %collective-permute-done.24.refs_2_, bf16[24,6144]{1,0:T(8,128)(2,1)S(1)} %copy-done.1, ...), custom_call_target="tpu_custom_call" | custom-call | flops 7247757312 | bytes 37748736 | tf_op jit(solution)/shard_map/cond/branch_1_fun/forward/pallas_call | solution.py:175
  78.3 16.1 %update.1 = bf16[1536,6144]{1,0:T(8,128)(2,1)} custom-call(f32[1]{0:T(128)} %bitcast.4.factor_ref, bf16[1536,6144]{1,0:T(8,128)(2,1)} %get-tuple-element.46.refs_17_.own_ref, bf16[192,1536]{1,0:T(8,128)(2,1)S(1)} %get-tuple-element.87.left_ref, bf16[192,6144]{1,0:T(8,128)(2,1)S(1)} %slice_bitcast_fusion.right_ref), custom_call_target="tpu_custom_call" | custom-call | flops 3623878656 | bytes 37748736 | tf_op jit(solution)/shard_map/cond/branch_1_fun/update/pallas_call | solution.py:306
  94.3 10.5 %fusion.11 = bf16[192,6144]{1,0:T(8,128)(2,1)S(1)} fusion(bf16[192,1536]{1,0:T(8,128)(2,1)S(1)} %get-tuple-element.62, bf16[6144,1536]{1,0:T(8,128)(2,1)} %get-tuple-element.55.refs_16_.own_ref), kind=kOutput, calls=%fused_computation.20 | convolution fusion | flops 3626237952 | bytes 21823488 | tf_op jit(solution)/shard_map/cond/branch_1_fun/dot_general | solution.py:121
  106.5 8.7 %fusion.24 = (bf16[384,6144]{1,0:T(8,128)(2,1)}, bf16[384,6144]{1,0:T(8,128)(2,1)}) fusion(bf16[1536,6144]{1,0:T(8,128)(2,1)} %update.1), kind=kLoop, calls=%fused_computation.50 | loop fusion | bytes 18874368 | tf_op jit(solution)/shard_map/cond/branch_1_fun/slice | solution.py:349
  115.2 300.9 %collective-permute-done.36 = bf16[24,6144]{1,0:T(8,128)(2,1)S(1)} collective-permute-done((bf16[24,6144]{1,0:T(8,128)(2,1)}, bf16[24,6144]{1,0:T(8,128)(2,1)S(1)}, u32[]{:S(2)}, u32[]{:S(2)}) %collective-permute-start.36) | collective-permute-done | bytes 294944 | tf_op jit(solution)/shard_map/cond/branch_1_fun/ppermute | solution.py:14
  425.1 3.9 slice.110
  433.2 8.4 collective-permute-done.41
  443.7 6.8 collective-permute-start.43
  452.1 4.9 collective-permute-done.43
  459.5 7.4 collective-permute-done.44
  468.3 52.8 %collective-permute-done.37 = bf16[384,6144]{1,0:T(8,128)(2,1)} collective-permute-done((bf16[384,6144]{1,0:T(8,128)(2,1)}, bf16[384,6144]{1,0:T(8,128)(2,1)}, u32[]{:S(2)}, u32[]{:S(2)}) %collective-permute-start.37) | collective-permute-done | bytes 4718624 | tf_op jit(solution)/shard_map/cond/branch_1_fun/ppermute | solution.py:14
  522.9 5.6 multiply_convert_fusion.2
  528.5 6.0 dynamic_update_slice.10
  534.5 87.7 %collective-permute-done.51 = bf16[384,6144]{1,0:T(8,128)(2,1)} collective-permute-done((bf16[384,6144]{1,0:T(8,128)(2,1)}, bf16[384,6144]{1,0:T(8,128)(2,1)}, u32[]{:S(2)}, u32[]{:S(2)}) %collective-permute-start.51) | collective-permute-done | bytes 4718624 | tf_op jit(solution)/shard_map/cond/branch_1_fun/ppermute | solution.py:14
  622.3 6.1 fusion.23
  632.8 5.2 collective-permute-done.48
  638.0 3.1 collective-permute-done.49
  641.2 24.8 %finish.5 = bf16[6144,1536]{1,0:T(8,128)(2,1)} custom-call(f32[1]{0:T(128)} %bitcast.7.factor_ref, bf16[6144,1536]{1,0:T(8,128)(2,1)} %get-tuple-element.55.refs_16_.own_ref, bf16[6144,1536]{1,0:T(8,128)(2,1)} %collective-permute-done.38.other_ref, bf16[2,192,6144]{2,1,0:T(8,128)(2,1)} %get-tuple-element.57.left_ref, bf16[1,192,6144]{2,1,0:T(8,128)(2,1)S(1)} %bitcast.32, ...), custom_call_target="tpu_custom_call" | custom-call | flops 7247757312 | bytes 56623104 | tf_op jit(solution)/shard_map/cond/branch_1_fun/finish/pallas_call | solution.py:226
  666.0 69.9 %collective-permute-done.52 = bf16[384,6144]{1,0:T(8,128)(2,1)S(1)} collective-permute-done((bf16[384,6144]{1,0:T(8,128)(2,1)S(1)}, bf16[384,6144]{1,0:T(8,128)(2,1)S(1)}, u32[]{:S(2)}, u32[]{:S(2)}) %collective-permute-start.52) | collective-permute-done | bytes 4718624 | tf_op jit(solution)/shard_map/cond/branch_1_fun/ppermute | solution.py:14
  737.7 6.1 fusion.13
  743.8 59.7 %collective-permute-done.53 = bf16[256,6144]{1,0:T(8,128)(2,1)} collective-permute-done((bf16[256,6144]{1,0:T(8,128)(2,1)}, bf16[256,6144]{1,0:T(8,128)(2,1)}, u32[]{:S(2)}, u32[]{:S(2)}) %collective-permute-start.53) | collective-permute-done | bytes 3145760 | tf_op jit(solution)/shard_map/cond/branch_1_fun/ppermute | solution.py:14
  803.4 5.7 fusion.14
  809.1 26.2 %collective-permute-done.54 = bf16[128,6144]{1,0:T(8,128)(2,1)S(1)} collective-permute-done((bf16[128,6144]{1,0:T(8,128)(2,1)S(1)}, bf16[128,6144]{1,0:T(8,128)(2,1)S(1)}, u32[]{:S(2)}, u32[]{:S(2)}) %collective-permute-start.54) | collective-permute-done | bytes 1572896 | tf_op jit(solution)/shard_map/cond/branch_1_fun/ppermute | solution.py:14
  835.3 3.0 fusion.15
  (100 shorter events, 63.6 us)
Async XLA Ops:
  1.4 423.2 %collective-permute-start.38 = (bf16[6144,1536]{1,0:T(8,128)(2,1)}, bf16[6144,1536]{1,0:T(8,128)(2,1)}, u32[]{:S(2)}, u32[]{:S(2)}) collective-permute-start(bf16[6144,1536]{1,0:T(8,128)(2,1)} %get-tuple-element.55.refs_16_.own_ref), channel_id=1, source_target_pairs={{0,16},{8,24},{16,0},{24,8},{1,17},{9,25},{17,1},{25,9},{2,18},{10... | collective-permute-start | bytes 56623112 | tf_op jit(solution)/shard_map/cond/branch_1_fun/ppermute | solution.py:14
  4.4 11.9 %collective-permute-start.22 = (bf16[24,6144]{1,0:T(8,128)(2,1)}, bf16[24,6144]{1,0:T(8,128)(2,1)S(1)}, u32[]{:S(2)}, u32[]{:S(2)}) collective-permute-start(bf16[24,6144]{1,0:T(8,128)(2,1)} %get-tuple-element.47.refs_0_), channel_id=1, source_target_pairs={{0,2},{1,3},{2,4},{3,5},{4,6},{5,7},{6,0},{7,1},{8,10},{9,11},{10,... | collective-permute-start | bytes 884744 | tf_op jit(solution)/shard_map/cond/branch_1_fun/ppermute | solution.py:33
  6.0 10.4 %collective-permute-start.23 = (bf16[24,6144]{1,0:T(8,128)(2,1)}, bf16[24,6144]{1,0:T(8,128)(2,1)S(1)}, u32[]{:S(2)}, u32[]{:S(2)}) collective-permute-start(bf16[24,6144]{1,0:T(8,128)(2,1)} %get-tuple-element.47.refs_0_), channel_id=1, source_target_pairs={{0,1},{1,0},{2,3},{3,2},{4,5},{5,4},{6,7},{7,6},{8,9},{9,8},{10,11... | collective-permute-start | bytes 884744 | tf_op jit(solution)/shard_map/cond/branch_1_fun/ppermute | solution.py:42
  7.5 15.2 %collective-permute-start.29 = (bf16[24,6144]{1,0:T(8,128)(2,1)}, bf16[24,6144]{1,0:T(8,128)(2,1)S(1)}, u32[]{:S(2)}, u32[]{:S(2)}) collective-permute-start(bf16[24,6144]{1,0:T(8,128)(2,1)} %get-tuple-element.51.refs_8_), channel_id=1, source_target_pairs={{0,2},{1,3},{2,4},{3,5},{4,6},{5,7},{6,0},{7,1},{8,10},{9,11},{10,... | collective-permute-start | bytes 884744 | tf_op jit(solution)/shard_map/cond/branch_1_fun/ppermute | solution.py:33
  9.0 13.6 %collective-permute-start.30 = (bf16[24,6144]{1,0:T(8,128)(2,1)}, bf16[24,6144]{1,0:T(8,128)(2,1)S(1)}, u32[]{:S(2)}, u32[]{:S(2)}) collective-permute-start(bf16[24,6144]{1,0:T(8,128)(2,1)} %get-tuple-element.51.refs_8_), channel_id=1, source_target_pairs={{0,1},{1,0},{2,3},{3,2},{4,5},{5,4},{6,7},{7,6},{8,9},{9,8},{10,11... | collective-permute-start | bytes 884744 | tf_op jit(solution)/shard_map/cond/branch_1_fun/ppermute | solution.py:42
  16.3 12.6 %collective-permute-start.24 = (bf16[24,6144]{1,0:T(8,128)(2,1)S(1)}, bf16[24,6144]{1,0:T(8,128)(2,1)S(1)}, u32[]{:S(2)}, u32[]{:S(2)}) collective-permute-start(bf16[24,6144]{1,0:T(8,128)(2,1)S(1)} %collective-permute-done.22.refs_1_), channel_id=1, source_target_pairs={{0,2},{1,3},{2,4},{3,5},{4,6},{5,7},{6,0},{7,1},{8,10},{9,11},{10,... | collective-permute-start | bytes 884744 | tf_op jit(solution)/shard_map/cond/branch_1_fun/ppermute | solution.py:33
  17.7 11.3 %collective-permute-start.25 = (bf16[24,6144]{1,0:T(8,128)(2,1)S(1)}, bf16[24,6144]{1,0:T(8,128)(2,1)S(1)}, u32[]{:S(2)}, u32[]{:S(2)}) collective-permute-start(bf16[24,6144]{1,0:T(8,128)(2,1)S(1)} %collective-permute-done.22.refs_1_), channel_id=1, source_target_pairs={{0,1},{1,0},{2,3},{3,2},{4,5},{5,4},{6,7},{7,6},{8,9},{9,8},{10,11... | collective-permute-start | bytes 884744 | tf_op jit(solution)/shard_map/cond/branch_1_fun/ppermute | solution.py:42
  22.6 12.6 %collective-permute-start.31 = (bf16[24,6144]{1,0:T(8,128)(2,1)S(1)}, bf16[24,6144]{1,0:T(8,128)(2,1)S(1)}, u32[]{:S(2)}, u32[]{:S(2)}) collective-permute-start(bf16[24,6144]{1,0:T(8,128)(2,1)S(1)} %collective-permute-done.29.refs_9_), channel_id=1, source_target_pairs={{0,2},{1,3},{2,4},{3,5},{4,6},{5,7},{6,0},{7,1},{8,10},{9,11},{10,... | collective-permute-start | bytes 884744 | tf_op jit(solution)/shard_map/cond/branch_1_fun/ppermute | solution.py:33
  24.0 11.3 %collective-permute-start.32 = (bf16[24,6144]{1,0:T(8,128)(2,1)S(1)}, bf16[24,6144]{1,0:T(8,128)(2,1)S(1)}, u32[]{:S(2)}, u32[]{:S(2)}) collective-permute-start(bf16[24,6144]{1,0:T(8,128)(2,1)S(1)} %collective-permute-done.29.refs_9_), channel_id=1, source_target_pairs={{0,1},{1,0},{2,3},{3,2},{4,5},{5,4},{6,7},{7,6},{8,9},{9,8},{10,11... | collective-permute-start | bytes 884744 | tf_op jit(solution)/shard_map/cond/branch_1_fun/ppermute | solution.py:42
  29.0 12.7 %collective-permute-start.26 = (bf16[24,6144]{1,0:T(8,128)(2,1)S(1)}, bf16[24,6144]{1,0:T(8,128)(2,1)S(1)}, u32[]{:S(2)}, u32[]{:S(2)}) collective-permute-start(bf16[24,6144]{1,0:T(8,128)(2,1)S(1)} %collective-permute-done.24.refs_2_), channel_id=1, source_target_pairs={{0,2},{1,3},{2,4},{3,5},{4,6},{5,7},{6,0},{7,1},{8,10},{9,11},{10,... | collective-permute-start | bytes 884744 | tf_op jit(solution)/shard_map/cond/branch_1_fun/ppermute | solution.py:33
  30.3 13.1 %collective-permute-start.27 = (bf16[24,6144]{1,0:T(8,128)(2,1)S(1)}, bf16[24,6144]{1,0:T(8,128)(2,1)S(1)}, u32[]{:S(2)}, u32[]{:S(2)}) collective-permute-start(bf16[24,6144]{1,0:T(8,128)(2,1)S(1)} %collective-permute-done.24.refs_2_), channel_id=1, source_target_pairs={{0,1},{1,0},{2,3},{3,2},{4,5},{5,4},{6,7},{7,6},{8,9},{9,8},{10,11... | collective-permute-start | bytes 884744 | tf_op jit(solution)/shard_map/cond/branch_1_fun/ppermute | solution.py:42
  35.3 12.7 %collective-permute-start.33 = (bf16[24,6144]{1,0:T(8,128)(2,1)S(1)}, bf16[24,6144]{1,0:T(8,128)(2,1)S(1)}, u32[]{:S(2)}, u32[]{:S(2)}) collective-permute-start(bf16[24,6144]{1,0:T(8,128)(2,1)S(1)} %collective-permute-done.31.refs_10_), channel_id=1, source_target_pairs={{0,2},{1,3},{2,4},{3,5},{4,6},{5,7},{6,0},{7,1},{8,10},{9,11},{10,... | collective-permute-start | bytes 884744 | tf_op jit(solution)/shard_map/cond/branch_1_fun/ppermute | solution.py:33
  36.7 12.3 %collective-permute-start.34 = (bf16[24,6144]{1,0:T(8,128)(2,1)S(1)}, bf16[24,6144]{1,0:T(8,128)(2,1)S(1)}, u32[]{:S(2)}, u32[]{:S(2)}) collective-permute-start(bf16[24,6144]{1,0:T(8,128)(2,1)S(1)} %collective-permute-done.31.refs_10_), channel_id=1, source_target_pairs={{0,1},{1,0},{2,3},{3,2},{4,5},{5,4},{6,7},{7,6},{8,9},{9,8},{10,11... | collective-permute-start | bytes 884744 | tf_op jit(solution)/shard_map/cond/branch_1_fun/ppermute | solution.py:42
  41.7 11.3 %collective-permute-start.35 = (bf16[24,6144]{1,0:T(8,128)(2,1)S(1)}, bf16[24,6144]{1,0:T(8,128)(2,1)}, u32[]{:S(2)}, u32[]{:S(2)}) collective-permute-start(bf16[24,6144]{1,0:T(8,128)(2,1)S(1)} %collective-permute-done.30.refs_12_), channel_id=1, source_target_pairs={{0,6},{1,7},{2,0},{3,1},{4,2},{5,3},{6,4},{7,5},{8,14},{9,15},{10,... | collective-permute-start | bytes 884744 | tf_op jit(solution)/shard_map/cond/branch_1_fun/ppermute | solution.py:38
  44.1 8.9 %collective-permute-start.28 = (bf16[24,6144]{1,0:T(8,128)(2,1)S(1)}, bf16[24,6144]{1,0:T(8,128)(2,1)S(1)}, u32[]{:S(2)}, u32[]{:S(2)}) collective-permute-start(bf16[24,6144]{1,0:T(8,128)(2,1)S(1)} %collective-permute-done.26.refs_3_), channel_id=1, source_target_pairs={{0,1},{1,0},{2,3},{3,2},{4,5},{5,4},{6,7},{7,6},{8,9},{9,8},{10,11... | collective-permute-start | bytes 884744 | tf_op jit(solution)/shard_map/cond/branch_1_fun/ppermute | solution.py:42
  48.7 367.4 %collective-permute-start.36 = (bf16[24,6144]{1,0:T(8,128)(2,1)}, bf16[24,6144]{1,0:T(8,128)(2,1)S(1)}, u32[]{:S(2)}, u32[]{:S(2)}) collective-permute-start(bf16[24,6144]{1,0:T(8,128)(2,1)} %get-tuple-element.47.refs_0_), channel_id=1, source_target_pairs={{0,16},{8,24},{16,0},{24,8},{1,17},{9,25},{17,1},{25,9},{2,18},{10... | collective-permute-start | bytes 884744 | tf_op jit(solution)/shard_map/cond/branch_1_fun/ppermute | solution.py:14
  104.9 312.9 %collective-permute-start.39 = (bf16[96,6144]{1,0:T(8,128)(2,1)S(1)}, bf16[96,6144]{1,0:T(8,128)(2,1)S(1)}, u32[]{:S(2)}, u32[]{:S(2)}) collective-permute-start(bf16[96,6144]{1,0:T(8,128)(2,1)S(1)} %slice.100), channel_id=1, source_target_pairs={{0,1},{1,0},{2,3},{3,2},{4,5},{5,4},{6,7},{7,6},{8,9},{9,8},{10,11... | collective-permute-start | bytes 3538952 | tf_op jit(solution)/shard_map/cond/branch_1_fun/ppermute | solution.py:42
  416.1 105.1 %collective-permute-start.37 = (bf16[384,6144]{1,0:T(8,128)(2,1)}, bf16[384,6144]{1,0:T(8,128)(2,1)}, u32[]{:S(2)}, u32[]{:S(2)}) collective-permute-start(bf16[384,6144]{1,0:T(8,128)(2,1)} %get-tuple-element.58), channel_id=1, source_target_pairs={{0,16},{8,24},{16,0},{24,8},{1,17},{9,25},{17,1},{25,9},{2,18},{10... | collective-permute-start | bytes 14155784 | tf_op jit(solution)/shard_map/cond/branch_1_fun/ppermute | solution.py:14
  419.1 12.6 %collective-permute-start.42 = (bf16[24,6144]{1,0:T(8,128)(2,1)}, bf16[24,6144]{1,0:T(8,128)(2,1)}, u32[]{:S(2)}, u32[]{:S(2)}) collective-permute-start(bf16[24,6144]{1,0:T(8,128)(2,1)} %get-tuple-element.84), channel_id=1, source_target_pairs={{0,2},{1,3},{2,4},{3,5},{4,6},{5,7},{6,0},{7,1},{8,10},{9,11},{10,... | collective-permute-start | bytes 884744 | tf_op jit(solution)/shard_map/cond/branch_1_fun/ppermute | solution.py:100
  420.6 21.0 %collective-permute-start.41 = (bf16[24,6144]{1,0:T(8,128)(2,1)}, bf16[24,6144]{1,0:T(8,128)(2,1)}, u32[]{:S(2)}, u32[]{:S(2)}) collective-permute-start(bf16[24,6144]{1,0:T(8,128)(2,1)} %get-tuple-element.85), channel_id=1, source_target_pairs={{0,4},{1,5},{2,6},{3,7},{4,0},{5,1},{6,2},{7,3},{8,12},{9,13},{10,... | collective-permute-start | bytes 884744 | tf_op jit(solution)/shard_map/cond/branch_1_fun/ppermute | solution.py:100
  423.2 18.4 %collective-permute-start.40 = (bf16[24,6144]{1,0:T(8,128)(2,1)}, bf16[24,6144]{1,0:T(8,128)(2,1)}, u32[]{:S(2)}, u32[]{:S(2)}) collective-permute-start(bf16[24,6144]{1,0:T(8,128)(2,1)} %get-tuple-element.83), channel_id=1, source_target_pairs={{0,6},{1,7},{2,0},{3,1},{4,2},{5,3},{6,4},{7,5},{8,14},{9,15},{10,... | collective-permute-start | bytes 884744 | tf_op jit(solution)/shard_map/cond/branch_1_fun/ppermute | solution.py:100
  424.6 197.7 %collective-permute-start.51 = (bf16[384,6144]{1,0:T(8,128)(2,1)}, bf16[384,6144]{1,0:T(8,128)(2,1)}, u32[]{:S(2)}, u32[]{:S(2)}) collective-permute-start(bf16[384,6144]{1,0:T(8,128)(2,1)} %get-tuple-element.63), channel_id=1, source_target_pairs={{0,16},{8,24},{16,0},{24,8},{1,17},{9,25},{17,1},{25,9},{2,18},{10... | collective-permute-start | bytes 14155784 | tf_op jit(solution)/shard_map/cond/branch_1_fun/ppermute | solution.py:14
  431.7 209.5 %collective-permute-start.50 = (bf16[192,1536]{1,0:T(8,128)(2,1)S(1)}, bf16[192,1536]{1,0:T(8,128)(2,1)S(1)}, u32[]{:S(2)}, u32[]{:S(2)}) collective-permute-start(bf16[192,1536]{1,0:T(8,128)(2,1)S(1)} %copy-done.17), channel_id=1, source_target_pairs={{0,16},{8,24},{16,0},{24,8},{1,17},{9,25},{17,1},{25,9},{2,18},{10... | collective-permute-start | bytes 1769480 | tf_op jit(solution)/shard_map/cond/branch_1_fun/ppermute | solution.py:14
  443.7 13.2 %collective-permute-start.43 = (bf16[24,6144]{1,0:T(8,128)(2,1)S(1)}, bf16[24,6144]{1,0:T(8,128)(2,1)S(1)}, u32[]{:S(2)}, u32[]{:S(2)}) collective-permute-start(bf16[24,6144]{1,0:T(8,128)(2,1)S(1)} %copy-done.19), channel_id=1, source_target_pairs={{0,2},{1,3},{2,4},{3,5},{4,6},{5,7},{6,0},{7,1},{8,10},{9,11},{10,... | collective-permute-start | bytes 884744 | tf_op jit(solution)/shard_map/cond/branch_1_fun/ppermute | solution.py:33
  450.5 181.2 %collective-permute-start.46 = (bf16[24,6144]{1,0:T(8,128)(2,1)S(1)}, bf16[24,6144]{1,0:T(8,128)(2,1)S(1)}, u32[]{:S(2)}, u32[]{:S(2)}) collective-permute-start(bf16[24,6144]{1,0:T(8,128)(2,1)S(1)} %copy-done.19), channel_id=1, source_target_pairs={{0,1},{1,0},{2,3},{3,2},{4,5},{5,4},{6,7},{7,6},{8,9},{9,8},{10,11... | collective-permute-start | bytes 884744 | tf_op jit(solution)/shard_map/cond/branch_1_fun/ppermute | solution.py:42
  457.0 9.9 %collective-permute-start.44 = (bf16[24,6144]{1,0:T(8,128)(2,1)S(1)}, bf16[24,6144]{1,0:T(8,128)(2,1)S(1)}, u32[]{:S(2)}, u32[]{:S(2)}) collective-permute-start(bf16[24,6144]{1,0:T(8,128)(2,1)S(1)} %collective-permute-done.43), channel_id=1, source_target_pairs={{0,2},{1,3},{2,4},{3,5},{4,6},{5,7},{6,0},{7,1},{8,10},{9,11},{10,... | collective-permute-start | bytes 884744 | tf_op jit(solution)/shard_map/cond/branch_1_fun/ppermute | solution.py:33
  466.9 165.5 %collective-permute-start.47 = (bf16[24,6144]{1,0:T(8,128)(2,1)S(1)}, bf16[24,6144]{1,0:T(8,128)(2,1)S(1)}, u32[]{:S(2)}, u32[]{:S(2)}) collective-permute-start(bf16[24,6144]{1,0:T(8,128)(2,1)S(1)} %collective-permute-done.43), channel_id=1, source_target_pairs={{0,1},{1,0},{2,3},{3,2},{4,5},{5,4},{6,7},{7,6},{8,9},{9,8},{10,11... | collective-permute-start | bytes 884744 | tf_op jit(solution)/shard_map/cond/branch_1_fun/ppermute | solution.py:42
  521.1 109.0 %collective-permute-start.45 = (bf16[24,6144]{1,0:T(8,128)(2,1)S(1)}, bf16[24,6144]{1,0:T(8,128)(2,1)S(1)}, u32[]{:S(2)}, u32[]{:S(2)}) collective-permute-start(bf16[24,6144]{1,0:T(8,128)(2,1)S(1)} %collective-permute-done.44), channel_id=1, source_target_pairs={{0,2},{1,3},{2,4},{3,5},{4,6},{5,7},{6,0},{7,1},{8,10},{9,11},{10,... | collective-permute-start | bytes 884744 | tf_op jit(solution)/shard_map/cond/branch_1_fun/ppermute | solution.py:33
  628.3 107.6 %collective-permute-start.52 = (bf16[384,6144]{1,0:T(8,128)(2,1)S(1)}, bf16[384,6144]{1,0:T(8,128)(2,1)S(1)}, u32[]{:S(2)}, u32[]{:S(2)}) collective-permute-start(bf16[384,6144]{1,0:T(8,128)(2,1)S(1)} %get-tuple-element.64), channel_id=1, source_target_pairs={{0,16},{8,24},{16,0},{24,8},{1,17},{9,25},{17,1},{25,9},{2,18},{10... | collective-permute-start | bytes 14155784 | tf_op jit(solution)/shard_map/cond/branch_1_fun/ppermute | solution.py:14
  631.8 9.4 %collective-permute-start.49 = (bf16[24,6144]{1,0:T(8,128)(2,1)S(1)}, bf16[24,6144]{1,0:T(8,128)(2,1)S(1)}, u32[]{:S(2)}, u32[]{:S(2)}) collective-permute-start(bf16[24,6144]{1,0:T(8,128)(2,1)S(1)} %collective-permute-done.45), channel_id=1, source_target_pairs={{0,1},{1,0},{2,3},{3,2},{4,5},{5,4},{6,7},{7,6},{8,9},{9,8},{10,11... | collective-permute-start | bytes 884744 | tf_op jit(solution)/shard_map/cond/branch_1_fun/ppermute | solution.py:42
  632.4 171.0 %collective-permute-start.53 = (bf16[256,6144]{1,0:T(8,128)(2,1)}, bf16[256,6144]{1,0:T(8,128)(2,1)}, u32[]{:S(2)}, u32[]{:S(2)}) collective-permute-start(bf16[256,6144]{1,0:T(8,128)(2,1)} %slice.110), channel_id=1, source_target_pairs={{0,16},{8,24},{16,0},{24,8},{1,17},{9,25},{17,1},{25,9},{2,18},{10... | collective-permute-start | bytes 9437192 | tf_op jit(solution)/shard_map/cond/branch_1_fun/ppermute | solution.py:14
  735.9 99.4 %collective-permute-start.54 = (bf16[128,6144]{1,0:T(8,128)(2,1)S(1)}, bf16[128,6144]{1,0:T(8,128)(2,1)S(1)}, u32[]{:S(2)}, u32[]{:S(2)}) collective-permute-start(bf16[128,6144]{1,0:T(8,128)(2,1)S(1)} %copy-done.15), channel_id=1, source_target_pairs={{0,16},{8,24},{16,0},{24,8},{1,17},{9,25},{17,1},{25,9},{2,18},{10... | collective-permute-start | bytes 4718600 | tf_op jit(solution)/shard_map/cond/branch_1_fun/ppermute | solution.py:14
  (20 other events, 513.3 us)

commit v2 on v1

--- a/solution.py
+++ b/solution.py
@@ -70,7 +70,7 @@
     ]
 
 
-def scatter_sum(partial_sums, rows, pieces=()):
+def scatter_sum(halves, rows, pieces=()):
     pieces, given = list(pieces), ()
 
     def work(gate, *arrived):
@@ -82,19 +82,22 @@
         return arrived
 
     if not short_ring():
-        done = lax.psum_scatter(partial_sums, "tp", scatter_dimension=0, tiled=True)
+        whole = jnp.concatenate(halves, axis=0)
+        done = lax.psum_scatter(whole, "tp", scatter_dimension=0, tiled=True)
         while pieces:
-            work(partial_sums)
+            work(halves[0])
         return done, given
     inner = flip_size()
     size = lax.axis_size("tp")
     ring = size // inner
-    slot = lambda number: partial_sums[number * rows : (number + 1) * rows]
+    straight = halves[0] if inner == 2 else jnp.concatenate(halves, axis=0)
+    slot = lambda number: straight[number * rows : (number + 1) * rows]
     sums = [slot(k).astype(jnp.float32) for k in range(ring)]
     if inner == 2:
-        (arrived,) = work(partial_sums, flip(partial_sums[ring * rows :]))
-        arrived = arrived.astype(jnp.float32).reshape(ring, rows, -1)
-        sums = [own + arrived[k] for k, own in enumerate(sums)]
+        (arrived,) = work(halves[0], flip(halves[1]))
+        sums = [
+            own + arrived[k * rows : (k + 1) * rows].astype(jnp.float32) for k, own in enumerate(sums)
+        ]
     leaving = [total.astype(jnp.bfloat16) for total in sums[1:]]
     arrived = [
         lax.ppermute(value, "tp", [(i, (i - k * inner) % size) for i in range(size)])
@@ -201,8 +204,50 @@
     )(*tok_slots, *up_slots, w_in, w_out)
 
 
-def finish_kernel(factor_ref, own_ref, other_ref, left_ref, left2_ref, right_ref, right2_ref, out_ref):
-    grad = dot_tn(left_ref[...], right_ref[...]) + dot_tn(left2_ref[...], right2_ref[...])
+def partial_kernel(dpre_ref, w_in_ref, first_ref, second_ref, *, scale_in):
+    sums = (dot_nt(dpre_ref[...], w_in_ref[...]) * scale_in).astype(jnp.bfloat16)
+    half = first_ref.shape[0]
+    first_ref[...] = sums[:half]
+    second_ref[...] = sums[half:]
+
+
+def partial_sums(both, w_in, scale_in):
+    _, rows, hid = both.shape
+    width, half, size = w_in.shape[0], rows // 2, 1024
+    if rows > 256 or width % size or half % 16:
+        whole = (dot_nt(both[1], w_in) * scale_in).astype(jnp.bfloat16)
+        return whole[:half], whole[half:]
+    part = pl.BlockSpec((half, size), lambda i: (0, i))
+    return pl.pallas_call(
+        partial(partial_kernel, scale_in=scale_in),
+        grid=(width // size,),
+        in_specs=[
+            pl.BlockSpec((None, rows, hid), lambda i: (1, 0, 0), pipeline_mode=pl.Buffered(1)),
+            pl.BlockSpec((size, hid), lambda i: (i, 0)),
+        ],
+        out_specs=[part, part],
+        out_shape=[jax.ShapeDtypeStruct((half, width), jnp.bfloat16)] * 2,
+        compiler_params=pltpu.CompilerParams(vmem_limit_bytes=32 << 20),
+        cost_estimate=pl.CostEstimate(
+            flops=2 * rows * width * hid, bytes_accessed=2 * width * hid, transcendentals=0
+        ),
+        name="partial_sums",
+    )(both, w_in)
+
+
+def finish_kernel(
+    factor_ref, own_ref, other_ref, left_ref, left2_ref, right_ref, right2_ref, out_ref, lefts_ref, rights_ref
+):
+    depth = left_ref.shape[0]
+
+    @pl.when(pl.program_id(0) == 0)
+    def _():
+        rights_ref[:depth] = right_ref[...]
+        rights_ref[depth:] = right2_ref[...]
+
+    lefts_ref[:depth] = left_ref[...]
+    lefts_ref[depth:] = left2_ref[...]
+    grad = dot_tn(lefts_ref[...], rights_ref[...])
     both = own_ref[...].astype(jnp.float32) + other_ref[...].astype(jnp.float32)
     out_ref[...] = (0.5 * both - factor_ref[0] * grad).astype(jnp.bfloat16)
 
@@ -235,6 +280,10 @@
         ],
         out_specs=tile,
         out_shape=jax.ShapeDtypeStruct(own.shape, jnp.bfloat16),
+        scratch_shapes=[
+            pltpu.VMEM((2 * depth, size), jnp.bfloat16),
+            pltpu.VMEM((2 * depth, width), jnp.bfloat16),
+        ],
         compiler_params=pltpu.CompilerParams(vmem_limit_bytes=48 << 20),
         cost_estimate=pl.CostEstimate(
             flops=4 * depth * width * count, bytes_accessed=6 * width * count, transcendentals=0
@@ -275,8 +324,8 @@
     both, sides = forward(tok_slots, up_slots, w_in, w_out, scale_in, scale_out)
     other_both = from_partner(both, bit)
     other_sides = from_partner(sides, bit)
-    partials = (dot_nt(both[1], w_in) * scale_in).astype(jnp.bfloat16)
-    other_out = from_partner(after(w_out, other_both, other_sides, partials), bit)
+    partials = partial_sums(both, w_in, scale_in)
+    other_out = from_partner(after(w_out, other_both, other_sides, *partials), bit)
     stacks = [
         (w_in, other_in, ((sides, 0), (other_sides, 0)), ((both, 1), (other_both, 1)), 0.5 * rate * scale_in),
         (w_out, other_out, ((both, 0), (other_both, 0)), ((sides, 1), (other_sides, 1)), 0.5 * rate * scale_out),
@@ -339,7 +388,7 @@
     dpre = both[1]
     dpre_other = from_partner(after(dpre, tok_other), bit)
     (new_out,) = update(w_out, both[0], sides[1], rate * scale_out, ((0, w_out.shape[1]),))
-    partials = (dot_nt(after(dpre, new_out), w_in) * scale_in).astype(jnp.bfloat16)
+    partials = partial_sums(after(both, new_out), w_in, scale_in)
     input_grad, _ = scatter_sum(partials, rows)
     tokens_other = gather_rows(after(tok_other, input_grad))[0]
     marks = [0, units // 4, units // 2, 3 * units // 4, units - 1, units]

time: 840 us -> 840 us (level)
  matrix products: 10.5 us -> 0 us
  Pallas kernels: 58.4 us -> 67.4 us
    pallas_call x0 -> x1, Pallas kernels: none -> 10.8 us  [partial_sums(): pl.pallas_call(partial(partial_kernel, scale_in=scale_in), grid=(width //...]
    dot_general x1 -> x0, matrix products: 10.5 us -> none  [dot_nt(): lax.dot_general(left, right, (((1,), (1,)), ((), ())), preferred_element_...]
  transfers between devices with their start and end apart: 33 -> 33, of which waited for: 18 -> 18; matrix products, arithmetic and copies ran while one was open for 7% -> 6% of each run, Pallas kernels for 7% -> 8%
where the time goes in v2:
time: 840 us; the launch traced here: 839 us
  waiting for transfers between devices  653 us (78%)
  Pallas kernels  67.4 us (8%)
  starting transfers between devices  54.1 us (6%)
  local copies, waits for them, and re-layouts  33.3 us (4%)
  other arithmetic  29.5 us (4%)
    ppermute x8, waiting for transfers between devices, from_partner(): return lax.ppermute(value, 'rep', pairs)  598 us
    ppermute x9, waiting for transfers between devices, step_up(): lax.ppermute(value, 'tp', [(i, (i + inner) % size) for i in range(size)])  34.6 us
    pallas_call x1, Pallas kernels, finish(): pl.pallas_call(finish_kernel, grid=(count // size,), in_specs=[pl.BlockSp...  23 us
    ppermute x9, starting transfers between devices, step_up(): lax.ppermute(value, 'tp', [(i, (i + inner) % size) for i in range(size)])  19.7 us
    pallas_call x1, Pallas kernels, forward(): pl.pallas_call(partial(forward_kernel, slots=slots, scale_in=scale_in, sc...  17.5 us
  transfers between devices with their start and end apart: 33, of which 18 were waited for; matrix products, arithmetic and copies ran while one was open for 6% of the time, Pallas kernels for 8%

profile of v2, /device:TPU:0, one launch (start us, length us, event | category | flops | bytes accessed | tf_op | source)
XLA Modules:
  0.0 839.0 jit_solution(2098812086713765105)
XLA Ops:
  1.3 837.0 %conditional.1 = (bf16[6144,1536]{1,0:T(8,128)(2,1)}, bf16[1536,6144]{1,0:T(8,128)(2,1)}, bf16[1,24,6144]{2,1,0:T(8,128)(2,1)S(1)}) conditional(s32[]{:T(128)} %clamp.3, (bf16[24,6144]{1,0:T(8,128)(2,1)}, bf16[6144,1536]{1,0:T(8,128)(2,1)}, bf16[24,6144]{1,0:T(8,128)(2,1)}, bf16[1536,6144]{1,0:T(8,128)(2,1)}, f32[]{:T(128)}) %tuple.61, (f32[]{:T(128)}, ...), branch_computations={%region_0.1_spmd, %region_1.2_spmd} | conditional | flops 25370394624 | bytes 572229120 | solution.py:420
  1.4 3.0 collective-permute-start.38
  9.6 6.8 collective-permute-done.22.refs_1_
  19.2 3.5 collective-permute-done.29.refs_9_
  25.5 3.5 collective-permute-done.24.refs_2_
  31.8 3.5 collective-permute-done.31.refs_10_
  38.2 3.5 collective-permute-done.26.refs_3_
  49.7 3.4 collective-permute-done.35.refs_15_
  58.6 17.5 %forward.3 = (bf16[2,192,1536]{2,1,0:T(8,128)(2,1)S(1)}, bf16[2,192,6144]{2,1,0:T(8,128)(2,1)}) custom-call(bf16[24,6144]{1,0:T(8,128)(2,1)} %get-tuple-element.49.refs_0_, bf16[24,6144]{1,0:T(8,128)(2,1)S(1)} %collective-permute-done.22.refs_1_, bf16[24,6144]{1,0:T(8,128)(2,1)S(1)} %collective-permute-done.24.refs_2_, bf16[24,6144]{1,0:T(8,128)(2,1)S(1)} %copy-done.1, ...), custom_call_target="tpu_custom_call" | custom-call | flops 7247757312 | bytes 37748736 | tf_op jit(solution)/shard_map/cond/branch_1_fun/forward/pallas_call | solution.py:178
  78.9 16.1 %update.1 = bf16[1536,6144]{1,0:T(8,128)(2,1)} custom-call(f32[1]{0:T(128)} %bitcast.3.factor_ref, bf16[1536,6144]{1,0:T(8,128)(2,1)} %get-tuple-element.48.refs_17_.own_ref, bf16[192,1536]{1,0:T(8,128)(2,1)S(1)} %get-tuple-element.91.left_ref, bf16[192,6144]{1,0:T(8,128)(2,1)S(1)} %slice_bitcast_fusion.right_ref), custom_call_target="tpu_custom_call" | custom-call | flops 3623878656 | bytes 37748736 | tf_op jit(solution)/shard_map/cond/branch_1_fun/update/pallas_call | solution.py:355
  95.0 10.8 %partial_sums.3 = (bf16[96,6144]{1,0:T(8,128)(2,1)S(1)}, bf16[96,6144]{1,0:T(8,128)(2,1)S(1)}) custom-call(bf16[2,192,1536]{2,1,0:T(8,128)(2,1)S(1)} %get-tuple-element.62.dpre_ref.right_ref, bf16[6144,1536]{1,0:T(8,128)(2,1)} %get-tuple-element.57.refs_16_.w_in_ref.own_ref), custom_call_target="tpu_custom_call" | custom-call | flops 3623878656 | bytes 18874368 | tf_op jit(solution)/shard_map/cond/branch_1_fun/partial_sums/pallas_call | solution.py:221
  107.3 8.7 %fusion.6 = (bf16[384,6144]{1,0:T(8,128)(2,1)}, bf16[384,6144]{1,0:T(8,128)(2,1)}) fusion(bf16[1536,6144]{1,0:T(8,128)(2,1)} %update.1), kind=kLoop, calls=%fused_computation.30 | loop fusion | bytes 18874368 | tf_op jit(solution)/shard_map/cond/branch_1_fun/slice | solution.py:398
  116.0 300.1 %collective-permute-done.36 = bf16[24,6144]{1,0:T(8,128)(2,1)S(1)} collective-permute-done((bf16[24,6144]{1,0:T(8,128)(2,1)}, bf16[24,6144]{1,0:T(8,128)(2,1)S(1)}, u32[]{:S(2)}, u32[]{:S(2)}) %collective-permute-start.36) | collective-permute-done | bytes 294944 | tf_op jit(solution)/shard_map/cond/branch_1_fun/ppermute | solution.py:14
  425.1 3.9 slice.79
  433.0 8.4 collective-permute-done.41
  443.4 6.8 collective-permute-start.43
  451.8 4.9 collective-permute-done.43
  459.2 7.4 collective-permute-done.44
  468.1 53.1 %collective-permute-done.37 = bf16[384,6144]{1,0:T(8,128)(2,1)} collective-permute-done((bf16[384,6144]{1,0:T(8,128)(2,1)}, bf16[384,6144]{1,0:T(8,128)(2,1)}, u32[]{:S(2)}, u32[]{:S(2)}) %collective-permute-start.37) | collective-permute-done | bytes 4718624 | tf_op jit(solution)/shard_map/cond/branch_1_fun/ppermute | solution.py:14
  522.9 5.6 multiply_convert_fusion.2
  528.5 6.0 dynamic_update_slice.10
  534.5 87.7 %collective-permute-done.51 = bf16[384,6144]{1,0:T(8,128)(2,1)} collective-permute-done((bf16[384,6144]{1,0:T(8,128)(2,1)}, bf16[384,6144]{1,0:T(8,128)(2,1)}, u32[]{:S(2)}, u32[]{:S(2)}) %collective-permute-start.51) | collective-permute-done | bytes 4718624 | tf_op jit(solution)/shard_map/cond/branch_1_fun/ppermute | solution.py:14
  622.3 6.1 fusion.5
  632.8 5.2 collective-permute-done.48
  638.0 3.1 collective-permute-done.49
  641.2 23.0 %finish.5 = bf16[6144,1536]{1,0:T(8,128)(2,1)} custom-call(f32[1]{0:T(128)} %bitcast.6.factor_ref, bf16[6144,1536]{1,0:T(8,128)(2,1)} %get-tuple-element.57.refs_16_.w_in_ref.own_ref, bf16[6144,1536]{1,0:T(8,128)(2,1)} %collective-permute-done.38.other_ref, bf16[2,192,6144]{2,1,0:T(8,128)(2,1)} %get-tuple-element.59.left_ref, ...), custom_call_target="tpu_custom_call" | custom-call | flops 7247757312 | bytes 56623104 | tf_op jit(solution)/shard_map/cond/branch_1_fun/finish/pallas_call | solution.py:271
  664.3 71.6 %collective-permute-done.52 = bf16[384,6144]{1,0:T(8,128)(2,1)S(1)} collective-permute-done((bf16[384,6144]{1,0:T(8,128)(2,1)S(1)}, bf16[384,6144]{1,0:T(8,128)(2,1)S(1)}, u32[]{:S(2)}, u32[]{:S(2)}) %collective-permute-start.52) | collective-permute-done | bytes 4718624 | tf_op jit(solution)/shard_map/cond/branch_1_fun/ppermute | solution.py:14
  737.7 6.1 fusion.2
  743.8 59.7 %collective-permute-done.53 = bf16[256,6144]{1,0:T(8,128)(2,1)} collective-permute-done((bf16[256,6144]{1,0:T(8,128)(2,1)}, bf16[256,6144]{1,0:T(8,128)(2,1)}, u32[]{:S(2)}, u32[]{:S(2)}) %collective-permute-start.53) | collective-permute-done | bytes 3145760 | tf_op jit(solution)/shard_map/cond/branch_1_fun/ppermute | solution.py:14
  803.4 5.7 fusion.3
  809.1 26.2 %collective-permute-done.54 = bf16[128,6144]{1,0:T(8,128)(2,1)S(1)} collective-permute-done((bf16[128,6144]{1,0:T(8,128)(2,1)S(1)}, bf16[128,6144]{1,0:T(8,128)(2,1)S(1)}, u32[]{:S(2)}, u32[]{:S(2)}) %collective-permute-start.54) | collective-permute-done | bytes 1572896 | tf_op jit(solution)/shard_map/cond/branch_1_fun/ppermute | solution.py:14
  835.3 3.0 fusion.4
  (94 shorter events, 63.8 us)
Async XLA Ops:
  1.4 423.0 %collective-permute-start.38 = (bf16[6144,1536]{1,0:T(8,128)(2,1)}, bf16[6144,1536]{1,0:T(8,128)(2,1)}, u32[]{:S(2)}, u32[]{:S(2)}) collective-permute-start(bf16[6144,1536]{1,0:T(8,128)(2,1)} %get-tuple-element.57.refs_16_.w_in_ref.own_ref), channel_id=1, source_target_pairs={{0,16},{8,24},{16,0},{24,8},{1,17},{9,25},{17,1},{25,9},{2,18},{10... | collective-permute-start | bytes 56623112 | tf_op jit(solution)/shard_map/cond/branch_1_fun/ppermute | solution.py:14
  4.4 11.9 %collective-permute-start.22 = (bf16[24,6144]{1,0:T(8,128)(2,1)}, bf16[24,6144]{1,0:T(8,128)(2,1)S(1)}, u32[]{:S(2)}, u32[]{:S(2)}) collective-permute-start(bf16[24,6144]{1,0:T(8,128)(2,1)} %get-tuple-element.49.refs_0_), channel_id=1, source_target_pairs={{0,2},{1,3},{2,4},{3,5},{4,6},{5,7},{6,0},{7,1},{8,10},{9,11},{10,... | collective-permute-start | bytes 884744 | tf_op jit(solution)/shard_map/cond/branch_1_fun/ppermute | solution.py:33
  6.0 10.4 %collective-permute-start.23 = (bf16[24,6144]{1,0:T(8,128)(2,1)}, bf16[24,6144]{1,0:T(8,128)(2,1)S(1)}, u32[]{:S(2)}, u32[]{:S(2)}) collective-permute-start(bf16[24,6144]{1,0:T(8,128)(2,1)} %get-tuple-element.49.refs_0_), channel_id=1, source_target_pairs={{0,1},{1,0},{2,3},{3,2},{4,5},{5,4},{6,7},{7,6},{8,9},{9,8},{10,11... | collective-permute-start | bytes 884744 | tf_op jit(solution)/shard_map/cond/branch_1_fun/ppermute | solution.py:42
  7.5 15.2 %collective-permute-start.29 = (bf16[24,6144]{1,0:T(8,128)(2,1)}, bf16[24,6144]{1,0:T(8,128)(2,1)S(1)}, u32[]{:S(2)}, u32[]{:S(2)}) collective-permute-start(bf16[24,6144]{1,0:T(8,128)(2,1)} %get-tuple-element.53.refs_8_), channel_id=1, source_target_pairs={{0,2},{1,3},{2,4},{3,5},{4,6},{5,7},{6,0},{7,1},{8,10},{9,11},{10,... | collective-permute-start | bytes 884744 | tf_op jit(solution)/shard_map/cond/branch_1_fun/ppermute | solution.py:33
  9.0 13.6 %collective-permute-start.30 = (bf16[24,6144]{1,0:T(8,128)(2,1)}, bf16[24,6144]{1,0:T(8,128)(2,1)S(1)}, u32[]{:S(2)}, u32[]{:S(2)}) collective-permute-start(bf16[24,6144]{1,0:T(8,128)(2,1)} %get-tuple-element.53.refs_8_), channel_id=1, source_target_pairs={{0,1},{1,0},{2,3},{3,2},{4,5},{5,4},{6,7},{7,6},{8,9},{9,8},{10,11... | collective-permute-start | bytes 884744 | tf_op jit(solution)/shard_map/cond/branch_1_fun/ppermute | solution.py:42
  16.3 12.6 %collective-permute-start.24 = (bf16[24,6144]{1,0:T(8,128)(2,1)S(1)}, bf16[24,6144]{1,0:T(8,128)(2,1)S(1)}, u32[]{:S(2)}, u32[]{:S(2)}) collective-permute-start(bf16[24,6144]{1,0:T(8,128)(2,1)S(1)} %collective-permute-done.22.refs_1_), channel_id=1, source_target_pairs={{0,2},{1,3},{2,4},{3,5},{4,6},{5,7},{6,0},{7,1},{8,10},{9,11},{10,... | collective-permute-start | bytes 884744 | tf_op jit(solution)/shard_map/cond/branch_1_fun/ppermute | solution.py:33
  17.7 11.3 %collective-permute-start.25 = (bf16[24,6144]{1,0:T(8,128)(2,1)S(1)}, bf16[24,6144]{1,0:T(8,128)(2,1)S(1)}, u32[]{:S(2)}, u32[]{:S(2)}) collective-permute-start(bf16[24,6144]{1,0:T(8,128)(2,1)S(1)} %collective-permute-done.22.refs_1_), channel_id=1, source_target_pairs={{0,1},{1,0},{2,3},{3,2},{4,5},{5,4},{6,7},{7,6},{8,9},{9,8},{10,11... | collective-permute-start | bytes 884744 | tf_op jit(solution)/shard_map/cond/branch_1_fun/ppermute | solution.py:42
  22.6 12.6 %collective-permute-start.31 = (bf16[24,6144]{1,0:T(8,128)(2,1)S(1)}, bf16[24,6144]{1,0:T(8,128)(2,1)S(1)}, u32[]{:S(2)}, u32[]{:S(2)}) collective-permute-start(bf16[24,6144]{1,0:T(8,128)(2,1)S(1)} %collective-permute-done.29.refs_9_), channel_id=1, source_target_pairs={{0,2},{1,3},{2,4},{3,5},{4,6},{5,7},{6,0},{7,1},{8,10},{9,11},{10,... | collective-permute-start | bytes 884744 | tf_op jit(solution)/shard_map/cond/branch_1_fun/ppermute | solution.py:33
  24.0 11.3 %collective-permute-start.32 = (bf16[24,6144]{1,0:T(8,128)(2,1)S(1)}, bf16[24,6144]{1,0:T(8,128)(2,1)S(1)}, u32[]{:S(2)}, u32[]{:S(2)}) collective-permute-start(bf16[24,6144]{1,0:T(8,128)(2,1)S(1)} %collective-permute-done.29.refs_9_), channel_id=1, source_target_pairs={{0,1},{1,0},{2,3},{3,2},{4,5},{5,4},{6,7},{7,6},{8,9},{9,8},{10,11... | collective-permute-start | bytes 884744 | tf_op jit(solution)/shard_map/cond/branch_1_fun/ppermute | solution.py:42
  29.0 12.7 %collective-permute-start.26 = (bf16[24,6144]{1,0:T(8,128)(2,1)S(1)}, bf16[24,6144]{1,0:T(8,128)(2,1)S(1)}, u32[]{:S(2)}, u32[]{:S(2)}) collective-permute-start(bf16[24,6144]{1,0:T(8,128)(2,1)S(1)} %collective-permute-done.24.refs_2_), channel_id=1, source_target_pairs={{0,2},{1,3},{2,4},{3,5},{4,6},{5,7},{6,0},{7,1},{8,10},{9,11},{10,... | collective-permute-start | bytes 884744 | tf_op jit(solution)/shard_map/cond/branch_1_fun/ppermute | solution.py:33
  30.3 13.1 %collective-permute-start.27 = (bf16[24,6144]{1,0:T(8,128)(2,1)S(1)}, bf16[24,6144]{1,0:T(8,128)(2,1)S(1)}, u32[]{:S(2)}, u32[]{:S(2)}) collective-permute-start(bf16[24,6144]{1,0:T(8,128)(2,1)S(1)} %collective-permute-done.24.refs_2_), channel_id=1, source_target_pairs={{0,1},{1,0},{2,3},{3,2},{4,5},{5,4},{6,7},{7,6},{8,9},{9,8},{10,11... | collective-permute-start | bytes 884744 | tf_op jit(solution)/shard_map/cond/branch_1_fun/ppermute | solution.py:42
  35.3 12.7 %collective-permute-start.33 = (bf16[24,6144]{1,0:T(8,128)(2,1)S(1)}, bf16[24,6144]{1,0:T(8,128)(2,1)S(1)}, u32[]{:S(2)}, u32[]{:S(2)}) collective-permute-start(bf16[24,6144]{1,0:T(8,128)(2,1)S(1)} %collective-permute-done.31.refs_10_), channel_id=1, source_target_pairs={{0,2},{1,3},{2,4},{3,5},{4,6},{5,7},{6,0},{7,1},{8,10},{9,11},{10,... | collective-permute-start | bytes 884744 | tf_op jit(solution)/shard_map/cond/branch_1_fun/ppermute | solution.py:33
  36.7 12.3 %collective-permute-start.34 = (bf16[24,6144]{1,0:T(8,128)(2,1)S(1)}, bf16[24,6144]{1,0:T(8,128)(2,1)S(1)}, u32[]{:S(2)}, u32[]{:S(2)}) collective-permute-start(bf16[24,6144]{1,0:T(8,128)(2,1)S(1)} %collective-permute-done.31.refs_10_), channel_id=1, source_target_pairs={{0,1},{1,0},{2,3},{3,2},{4,5},{5,4},{6,7},{7,6},{8,9},{9,8},{10,11... | collective-permute-start | bytes 884744 | tf_op jit(solution)/shard_map/cond/branch_1_fun/ppermute | solution.py:42
  41.7 11.3 %collective-permute-start.35 = (bf16[24,6144]{1,0:T(8,128)(2,1)S(1)}, bf16[24,6144]{1,0:T(8,128)(2,1)}, u32[]{:S(2)}, u32[]{:S(2)}) collective-permute-start(bf16[24,6144]{1,0:T(8,128)(2,1)S(1)} %collective-permute-done.30.refs_12_), channel_id=1, source_target_pairs={{0,6},{1,7},{2,0},{3,1},{4,2},{5,3},{6,4},{7,5},{8,14},{9,15},{10,... | collective-permute-start | bytes 884744 | tf_op jit(solution)/shard_map/cond/branch_1_fun/ppermute | solution.py:38
  44.1 8.9 %collective-permute-start.28 = (bf16[24,6144]{1,0:T(8,128)(2,1)S(1)}, bf16[24,6144]{1,0:T(8,128)(2,1)S(1)}, u32[]{:S(2)}, u32[]{:S(2)}) collective-permute-start(bf16[24,6144]{1,0:T(8,128)(2,1)S(1)} %collective-permute-done.26.refs_3_), channel_id=1, source_target_pairs={{0,1},{1,0},{2,3},{3,2},{4,5},{5,4},{6,7},{7,6},{8,9},{9,8},{10,11... | collective-permute-start | bytes 884744 | tf_op jit(solution)/shard_map/cond/branch_1_fun/ppermute | solution.py:42
  48.7 367.4 %collective-permute-start.36 = (bf16[24,6144]{1,0:T(8,128)(2,1)}, bf16[24,6144]{1,0:T(8,128)(2,1)S(1)}, u32[]{:S(2)}, u32[]{:S(2)}) collective-permute-start(bf16[24,6144]{1,0:T(8,128)(2,1)} %get-tuple-element.49.refs_0_), channel_id=1, source_target_pairs={{0,16},{8,24},{16,0},{24,8},{1,17},{9,25},{17,1},{25,9},{2,18},{10... | collective-permute-start | bytes 884744 | tf_op jit(solution)/shard_map/cond/branch_1_fun/ppermute | solution.py:14
  105.8 312.1 %collective-permute-start.39 = (bf16[96,6144]{1,0:T(8,128)(2,1)S(1)}, bf16[96,6144]{1,0:T(8,128)(2,1)S(1)}, u32[]{:S(2)}, u32[]{:S(2)}) collective-permute-start(bf16[96,6144]{1,0:T(8,128)(2,1)S(1)} %get-tuple-element.64), channel_id=1, source_target_pairs={{0,1},{1,0},{2,3},{3,2},{4,5},{5,4},{6,7},{7,6},{8,9},{9,8},{10,11... | collective-permute-start | bytes 3538952 | tf_op jit(solution)/shard_map/cond/branch_1_fun/ppermute | solution.py:42
  416.1 105.1 %collective-permute-start.37 = (bf16[384,6144]{1,0:T(8,128)(2,1)}, bf16[384,6144]{1,0:T(8,128)(2,1)}, u32[]{:S(2)}, u32[]{:S(2)}) collective-permute-start(bf16[384,6144]{1,0:T(8,128)(2,1)} %get-tuple-element.60), channel_id=1, source_target_pairs={{0,16},{8,24},{16,0},{24,8},{1,17},{9,25},{17,1},{25,9},{2,18},{10... | collective-permute-start | bytes 14155784 | tf_op jit(solution)/shard_map/cond/branch_1_fun/ppermute | solution.py:14
  418.9 12.9 %collective-permute-start.42 = (bf16[24,6144]{1,0:T(8,128)(2,1)}, bf16[24,6144]{1,0:T(8,128)(2,1)}, u32[]{:S(2)}, u32[]{:S(2)}) collective-permute-start(bf16[24,6144]{1,0:T(8,128)(2,1)} %get-tuple-element.88), channel_id=1, source_target_pairs={{0,2},{1,3},{2,4},{3,5},{4,6},{5,7},{6,0},{7,1},{8,10},{9,11},{10,... | collective-permute-start | bytes 884744 | tf_op jit(solution)/shard_map/cond/branch_1_fun/ppermute | solution.py:103
  420.4 21.0 %collective-permute-start.41 = (bf16[24,6144]{1,0:T(8,128)(2,1)}, bf16[24,6144]{1,0:T(8,128)(2,1)}, u32[]{:S(2)}, u32[]{:S(2)}) collective-permute-start(bf16[24,6144]{1,0:T(8,128)(2,1)} %get-tuple-element.89), channel_id=1, source_target_pairs={{0,4},{1,5},{2,6},{3,7},{4,0},{5,1},{6,2},{7,3},{8,12},{9,13},{10,... | collective-permute-start | bytes 884744 | tf_op jit(solution)/shard_map/cond/branch_1_fun/ppermute | solution.py:103
  423.0 18.4 %collective-permute-start.40 = (bf16[24,6144]{1,0:T(8,128)(2,1)}, bf16[24,6144]{1,0:T(8,128)(2,1)}, u32[]{:S(2)}, u32[]{:S(2)}) collective-permute-start(bf16[24,6144]{1,0:T(8,128)(2,1)} %get-tuple-element.87), channel_id=1, source_target_pairs={{0,6},{1,7},{2,0},{3,1},{4,2},{5,3},{6,4},{7,5},{8,14},{9,15},{10,... | collective-permute-start | bytes 884744 | tf_op jit(solution)/shard_map/cond/branch_1_fun/ppermute | solution.py:103
  424.4 197.9 %collective-permute-start.51 = (bf16[384,6144]{1,0:T(8,128)(2,1)}, bf16[384,6144]{1,0:T(8,128)(2,1)}, u32[]{:S(2)}, u32[]{:S(2)}) collective-permute-start(bf16[384,6144]{1,0:T(8,128)(2,1)} %get-tuple-element.67), channel_id=1, source_target_pairs={{0,16},{8,24},{16,0},{24,8},{1,17},{9,25},{17,1},{25,9},{2,18},{10... | collective-permute-start | bytes 14155784 | tf_op jit(solution)/shard_map/cond/branch_1_fun/ppermute | solution.py:14
  431.7 209.5 %collective-permute-start.50 = (bf16[192,1536]{1,0:T(8,128)(2,1)S(1)}, bf16[192,1536]{1,0:T(8,128)(2,1)S(1)}, u32[]{:S(2)}, u32[]{:S(2)}) collective-permute-start(bf16[192,1536]{1,0:T(8,128)(2,1)S(1)} %copy-done.13), channel_id=1, source_target_pairs={{0,16},{8,24},{16,0},{24,8},{1,17},{9,25},{17,1},{25,9},{2,18},{10... | collective-permute-start | bytes 1769480 | tf_op jit(solution)/shard_map/cond/branch_1_fun/ppermute | solution.py:14
  443.4 13.2 %collective-permute-start.43 = (bf16[24,6144]{1,0:T(8,128)(2,1)S(1)}, bf16[24,6144]{1,0:T(8,128)(2,1)S(1)}, u32[]{:S(2)}, u32[]{:S(2)}) collective-permute-start(bf16[24,6144]{1,0:T(8,128)(2,1)S(1)} %copy-done.17), channel_id=1, source_target_pairs={{0,2},{1,3},{2,4},{3,5},{4,6},{5,7},{6,0},{7,1},{8,10},{9,11},{10,... | collective-permute-start | bytes 884744 | tf_op jit(solution)/shard_map/cond/branch_1_fun/ppermute | solution.py:33
  450.3 181.5 %collective-permute-start.46 = (bf16[24,6144]{1,0:T(8,128)(2,1)S(1)}, bf16[24,6144]{1,0:T(8,128)(2,1)S(1)}, u32[]{:S(2)}, u32[]{:S(2)}) collective-permute-start(bf16[24,6144]{1,0:T(8,128)(2,1)S(1)} %copy-done.17), channel_id=1, source_target_pairs={{0,1},{1,0},{2,3},{3,2},{4,5},{5,4},{6,7},{7,6},{8,9},{9,8},{10,11... | collective-permute-start | bytes 884744 | tf_op jit(solution)/shard_map/cond/branch_1_fun/ppermute | solution.py:42
  456.7 9.9 %collective-permute-start.44 = (bf16[24,6144]{1,0:T(8,128)(2,1)S(1)}, bf16[24,6144]{1,0:T(8,128)(2,1)S(1)}, u32[]{:S(2)}, u32[]{:S(2)}) collective-permute-start(bf16[24,6144]{1,0:T(8,128)(2,1)S(1)} %collective-permute-done.43), channel_id=1, source_target_pairs={{0,2},{1,3},{2,4},{3,5},{4,6},{5,7},{6,0},{7,1},{8,10},{9,11},{10,... | collective-permute-start | bytes 884744 | tf_op jit(solution)/shard_map/cond/branch_1_fun/ppermute | solution.py:33
  466.6 165.8 %collective-permute-start.47 = (bf16[24,6144]{1,0:T(8,128)(2,1)S(1)}, bf16[24,6144]{1,0:T(8,128)(2,1)S(1)}, u32[]{:S(2)}, u32[]{:S(2)}) collective-permute-start(bf16[24,6144]{1,0:T(8,128)(2,1)S(1)} %collective-permute-done.43), channel_id=1, source_target_pairs={{0,1},{1,0},{2,3},{3,2},{4,5},{5,4},{6,7},{7,6},{8,9},{9,8},{10,11... | collective-permute-start | bytes 884744 | tf_op jit(solution)/shard_map/cond/branch_1_fun/ppermute | solution.py:42
  521.1 109.0 %collective-permute-start.45 = (bf16[24,6144]{1,0:T(8,128)(2,1)S(1)}, bf16[24,6144]{1,0:T(8,128)(2,1)S(1)}, u32[]{:S(2)}, u32[]{:S(2)}) collective-permute-start(bf16[24,6144]{1,0:T(8,128)(2,1)S(1)} %collective-permute-done.44), channel_id=1, source_target_pairs={{0,2},{1,3},{2,4},{3,5},{4,6},{5,7},{6,0},{7,1},{8,10},{9,11},{10,... | collective-permute-start | bytes 884744 | tf_op jit(solution)/shard_map/cond/branch_1_fun/ppermute | solution.py:33
  628.3 107.6 %collective-permute-start.52 = (bf16[384,6144]{1,0:T(8,128)(2,1)S(1)}, bf16[384,6144]{1,0:T(8,128)(2,1)S(1)}, u32[]{:S(2)}, u32[]{:S(2)}) collective-permute-start(bf16[384,6144]{1,0:T(8,128)(2,1)S(1)} %get-tuple-element.68), channel_id=1, source_target_pairs={{0,16},{8,24},{16,0},{24,8},{1,17},{9,25},{17,1},{25,9},{2,18},{10... | collective-permute-start | bytes 14155784 | tf_op jit(solution)/shard_map/cond/branch_1_fun/ppermute | solution.py:14
  631.8 9.4 %collective-permute-start.49 = (bf16[24,6144]{1,0:T(8,128)(2,1)S(1)}, bf16[24,6144]{1,0:T(8,128)(2,1)S(1)}, u32[]{:S(2)}, u32[]{:S(2)}) collective-permute-start(bf16[24,6144]{1,0:T(8,128)(2,1)S(1)} %collective-permute-done.45), channel_id=1, source_target_pairs={{0,1},{1,0},{2,3},{3,2},{4,5},{5,4},{6,7},{7,6},{8,9},{9,8},{10,11... | collective-permute-start | bytes 884744 | tf_op jit(solution)/shard_map/cond/branch_1_fun/ppermute | solution.py:42
  632.4 171.0 %collective-permute-start.53 = (bf16[256,6144]{1,0:T(8,128)(2,1)}, bf16[256,6144]{1,0:T(8,128)(2,1)}, u32[]{:S(2)}, u32[]{:S(2)}) collective-permute-start(bf16[256,6144]{1,0:T(8,128)(2,1)} %slice.79), channel_id=1, source_target_pairs={{0,16},{8,24},{16,0},{24,8},{1,17},{9,25},{17,1},{25,9},{2,18},{10... | collective-permute-start | bytes 9437192 | tf_op jit(solution)/shard_map/cond/branch_1_fun/ppermute | solution.py:14
  735.9 99.4 %collective-permute-start.54 = (bf16[128,6144]{1,0:T(8,128)(2,1)S(1)}, bf16[128,6144]{1,0:T(8,128)(2,1)S(1)}, u32[]{:S(2)}, u32[]{:S(2)}) collective-permute-start(bf16[128,6144]{1,0:T(8,128)(2,1)S(1)} %copy-done.12), channel_id=1, source_target_pairs={{0,16},{8,24},{16,0},{24,8},{1,17},{9,25},{17,1},{25,9},{2,18},{10... | collective-permute-start | bytes 4718600 | tf_op jit(solution)/shard_map/cond/branch_1_fun/ppermute | solution.py:14
  (18 other events, 180.4 us)

commit v3 on v2

--- a/solution.py
+++ b/solution.py
@@ -392,7 +392,9 @@
     input_grad, _ = scatter_sum(partials, rows)
     tokens_other = gather_rows(after(tok_other, input_grad))[0]
     marks = [0, units // 4, units // 2, 3 * units // 4, units - 1, units]
-    cuts = [(lo * unit, hi * unit) for lo, hi in zip(marks, marks[1:]) if lo < hi]
+    marks = [mark * unit for mark in marks]
+    marks[-2] += unit // 2
+    cuts = [(lo, hi) for lo, hi in zip(marks, marks[1:]) if lo < hi]
     mixed_in, mixed_out = None, jnp.zeros_like(w_out)
     for number, (lo, hi) in enumerate(cuts):
         own = new_out[lo:hi]

time: 840 us -> 143 us (0.17)
  waiting for transfers between devices: 653 us -> 32.5 us
  local copies, waits for them, and re-layouts: 33.3 us -> 0.71 us
  other arithmetic: 29.5 us -> 2.5 us
  starting transfers between devices: 54.1 us -> 28.5 us
  Pallas kernels: 67.4 us -> 76.6 us
    ppermute x8 -> x4, waiting for transfers between devices: 598 us -> 0.01 us  [from_partner(): return lax.ppermute(value, 'rep', pairs)]
    pallas_call x1 -> x2, Pallas kernels: 23 us -> 47.6 us  [finish(): pl.pallas_call(finish_kernel, grid=(count // size,), in_specs=[pl.BlockSp...]
    pallas_call x1 -> x0, Pallas kernels: 16.1 us -> none  [update(): pl.pallas_call(partial(update_kernel, cuts=cuts), grid=(count // size,),...]
    slice x3 -> x0, local copies, waits for them, and re-layouts: 15.3 us -> none  [far(): own = new_out[lo:hi]]
    dynamic_update_slice x3 -> x0, other arithmetic: 14.8 us -> none  [far(): lax.dynamic_update_slice(mixed_out, mean_of(own, other), (lo, 0))]
    ppermute x9 -> x6, waiting for transfers between devices: 34.6 us -> 22.6 us  [step_up(): lax.ppermute(value, 'tp', [(i, (i + inner) % size) for i in range(size)])]
    ppermute x8 -> x4, starting transfers between devices: 11 us -> 1.23 us  [from_partner(): return lax.ppermute(value, 'rep', pairs)]
    ppermute x9 -> x6, starting transfers between devices: 19.7 us -> 10.4 us  [step_up(): lax.ppermute(value, 'tp', [(i, (i + inner) % size) for i in range(size)])]
  transfers between devices with their start and end apart: 33 -> 22, of which waited for: 18 -> 8; matrix products, arithmetic and copies ran while one was open for 6% -> 1% of each run, Pallas kernels for 8% -> 42%
where the time goes in v3:
time: 143 us; the launch traced here: 142 us
  Pallas kernels  76.6 us (54%)
  waiting for transfers between devices  32.5 us (23%)
  starting transfers between devices  28.5 us (20%)
  other arithmetic  2.5 us (2%)
    pallas_call x2, Pallas kernels, finish(): pl.pallas_call(finish_kernel, grid=(count // size,), in_specs=[pl.BlockSp...  47.6 us
    ppermute x6, waiting for transfers between devices, step_up(): lax.ppermute(value, 'tp', [(i, (i + inner) % size) for i in range(size)])  22.6 us
    pallas_call x1, Pallas kernels, forward(): pl.pallas_call(partial(forward_kernel, slots=slots, scale_in=scale_in, sc...  17.5 us
    pallas_call x1, Pallas kernels, partial_sums(): pl.pallas_call(partial(partial_kernel, scale_in=scale_in), grid=(width //...  11.6 us
    ppermute x8, starting transfers between devices, flip(): lax.ppermute(value, 'tp', [(i, i ^ 1) for i in range(lax.axis_size('tp'))])  11 us
    ppermute x6, starting transfers between devices, step_up(): lax.ppermute(value, 'tp', [(i, (i + inner) % size) for i in range(size)])  10.4 us
    ppermute x1, waiting for transfers between devices, step_down(): lax.ppermute(value, 'tp', [(i, (i - inner) % size) for i in range(size)])  6.07 us
    ppermute x3, starting transfers between devices, scatter_sum(): lax.ppermute(value, 'tp', [(i, (i - k * inner) % size) for i in range(siz...  4 us
  transfers between devices with their start and end apart: 22, of which 8 were waited for; matrix products, arithmetic and copies ran while one was open for 1% of the time, Pallas kernels for 42%

profile of v3, /device:TPU:0, one launch (start us, length us, event | category | flops | bytes accessed | tf_op | source)
XLA Modules:
  0.0 142.5 jit_solution(11001867999533699248)
XLA Ops:
  1.3 140.4 %conditional.1 = (bf16[6144,1536]{1,0:T(8,128)(2,1)}, bf16[1536,6144]{1,0:T(8,128)(2,1)}, bf16[1,24,6144]{2,1,0:T(8,128)(2,1)S(1)}) conditional(s32[]{:T(128)} %clamp.3, (bf16[24,6144]{1,0:T(8,128)(2,1)}, bf16[6144,1536]{1,0:T(8,128)(2,1)}, bf16[24,6144]{1,0:T(8,128)(2,1)}, bf16[1536,6144]{1,0:T(8,128)(2,1)}, f32[]{:T(128)}) %tuple.61, (f32[]{:T(128)}, ...), branch_computations={%region_0.1_spmd, %region_1.2_spmd} | conditional | flops 25370394624 | bytes 569083392 | solution.py:422
  1.9 2.6 %collective-permute-start = (bf16[24,6144]{1,0:T(8,128)(2,1)}, bf16[24,6144]{1,0:T(8,128)(2,1)S(1)}, u32[]{:S(2)}, u32[]{:S(2)}) collective-permute-start(bf16[24,6144]{1,0:T(8,128)(2,1)} %get-tuple-element.21.refs_0_), channel_id=1, source_target_pairs={{0,2},{1,3},{2,4},{3,5},{4,6},{5,7},{6,0},{7,1},{8,10},{9,11},{10,... | collective-permute-start | bytes 884744 | tf_op jit(solution)/shard_map/cond/branch_0_fun/ppermute | solution.py:33
  4.5 1.5 %collective-permute-start.1 = (bf16[24,6144]{1,0:T(8,128)(2,1)}, bf16[24,6144]{1,0:T(8,128)(2,1)S(1)}, u32[]{:S(2)}, u32[]{:S(2)}) collective-permute-start(bf16[24,6144]{1,0:T(8,128)(2,1)} %get-tuple-element.21.refs_0_), channel_id=1, source_target_pairs={{0,1},{1,0},{2,3},{3,2},{4,5},{5,4},{6,7},{7,6},{8,9},{9,8},{10,11... | collective-permute-start | bytes 884744 | tf_op jit(solution)/shard_map/cond/branch_0_fun/ppermute | solution.py:42
  6.0 1.6 %collective-permute-start.8 = (bf16[24,6144]{1,0:T(8,128)(2,1)}, bf16[24,6144]{1,0:T(8,128)(2,1)S(1)}, u32[]{:S(2)}, u32[]{:S(2)}) collective-permute-start(bf16[24,6144]{1,0:T(8,128)(2,1)} %get-tuple-element.27.refs_8_), channel_id=1, source_target_pairs={{0,2},{1,3},{2,4},{3,5},{4,6},{5,7},{6,0},{7,1},{8,10},{9,11},{10,... | collective-permute-start | bytes 884744 | tf_op jit(solution)/shard_map/cond/branch_0_fun/ppermute | solution.py:33
  8.1 6.5 %collective-permute-done.refs_1_ = bf16[24,6144]{1,0:T(8,128)(2,1)S(1)} collective-permute-done((bf16[24,6144]{1,0:T(8,128)(2,1)}, bf16[24,6144]{1,0:T(8,128)(2,1)S(1)}, u32[]{:S(2)}, u32[]{:S(2)}) %collective-permute-start) | collective-permute-done | bytes 294944 | tf_op jit(solution)/shard_map/cond/branch_0_fun/ppermute | solution.py:33
  14.6 1.5 %collective-permute-start.2 = (bf16[24,6144]{1,0:T(8,128)(2,1)S(1)}, bf16[24,6144]{1,0:T(8,128)(2,1)S(1)}, u32[]{:S(2)}, u32[]{:S(2)}) collective-permute-start(bf16[24,6144]{1,0:T(8,128)(2,1)S(1)} %collective-permute-done.refs_1_), channel_id=1, source_target_pairs={{0,2},{1,3},{2,4},{3,5},{4,6},{5,7},{6,0},{7,1},{8,10},{9,11},{10,... | collective-permute-start | bytes 884744 | tf_op jit(solution)/shard_map/cond/branch_0_fun/ppermute | solution.py:33
  16.1 1.5 %collective-permute-start.3 = (bf16[24,6144]{1,0:T(8,128)(2,1)S(1)}, bf16[24,6144]{1,0:T(8,128)(2,1)S(1)}, u32[]{:S(2)}, u32[]{:S(2)}) collective-permute-start(bf16[24,6144]{1,0:T(8,128)(2,1)S(1)} %collective-permute-done.refs_1_), channel_id=1, source_target_pairs={{0,1},{1,0},{2,3},{3,2},{4,5},{5,4},{6,7},{7,6},{8,9},{9,8},{10,11... | collective-permute-start | bytes 884744 | tf_op jit(solution)/shard_map/cond/branch_0_fun/ppermute | solution.py:42
  17.6 3.3 %collective-permute-done.8.refs_9_ = bf16[24,6144]{1,0:T(8,128)(2,1)S(1)} collective-permute-done((bf16[24,6144]{1,0:T(8,128)(2,1)}, bf16[24,6144]{1,0:T(8,128)(2,1)S(1)}, u32[]{:S(2)}, u32[]{:S(2)}) %collective-permute-start.8) | collective-permute-done | bytes 294944 | tf_op jit(solution)/shard_map/cond/branch_0_fun/ppermute | solution.py:33
  20.9 1.5 %collective-permute-start.10 = (bf16[24,6144]{1,0:T(8,128)(2,1)S(1)}, bf16[24,6144]{1,0:T(8,128)(2,1)S(1)}, u32[]{:S(2)}, u32[]{:S(2)}) collective-permute-start(bf16[24,6144]{1,0:T(8,128)(2,1)S(1)} %collective-permute-done.8.refs_9_), channel_id=1, source_target_pairs={{0,2},{1,3},{2,4},{3,5},{4,6},{5,7},{6,0},{7,1},{8,10},{9,11},{10,... | collective-permute-start | bytes 884744 | tf_op jit(solution)/shard_map/cond/branch_0_fun/ppermute | solution.py:33
  22.5 1.5 %collective-permute-start.11 = (bf16[24,6144]{1,0:T(8,128)(2,1)S(1)}, bf16[24,6144]{1,0:T(8,128)(2,1)S(1)}, u32[]{:S(2)}, u32[]{:S(2)}) collective-permute-start(bf16[24,6144]{1,0:T(8,128)(2,1)S(1)} %collective-permute-done.8.refs_9_), channel_id=1, source_target_pairs={{0,1},{1,0},{2,3},{3,2},{4,5},{5,4},{6,7},{7,6},{8,9},{9,8},{10,11... | collective-permute-start | bytes 884744 | tf_op jit(solution)/shard_map/cond/branch_0_fun/ppermute | solution.py:42
  24.0 3.3 %collective-permute-done.2.refs_2_ = bf16[24,6144]{1,0:T(8,128)(2,1)S(1)} collective-permute-done((bf16[24,6144]{1,0:T(8,128)(2,1)S(1)}, bf16[24,6144]{1,0:T(8,128)(2,1)S(1)}, u32[]{:S(2)}, u32[]{:S(2)}) %collective-permute-start.2) | collective-permute-done | bytes 294944 | tf_op jit(solution)/shard_map/cond/branch_0_fun/ppermute | solution.py:33
  27.2 1.5 %collective-permute-start.4 = (bf16[24,6144]{1,0:T(8,128)(2,1)S(1)}, bf16[24,6144]{1,0:T(8,128)(2,1)S(1)}, u32[]{:S(2)}, u32[]{:S(2)}) collective-permute-start(bf16[24,6144]{1,0:T(8,128)(2,1)S(1)} %collective-permute-done.2.refs_2_), channel_id=1, source_target_pairs={{0,2},{1,3},{2,4},{3,5},{4,6},{5,7},{6,0},{7,1},{8,10},{9,11},{10,... | collective-permute-start | bytes 884744 | tf_op jit(solution)/shard_map/cond/branch_0_fun/ppermute | solution.py:33
  28.8 1.5 %collective-permute-start.5 = (bf16[24,6144]{1,0:T(8,128)(2,1)S(1)}, bf16[24,6144]{1,0:T(8,128)(2,1)S(1)}, u32[]{:S(2)}, u32[]{:S(2)}) collective-permute-start(bf16[24,6144]{1,0:T(8,128)(2,1)S(1)} %collective-permute-done.2.refs_2_), channel_id=1, source_target_pairs={{0,1},{1,0},{2,3},{3,2},{4,5},{5,4},{6,7},{7,6},{8,9},{9,8},{10,11... | collective-permute-start | bytes 884744 | tf_op jit(solution)/shard_map/cond/branch_0_fun/ppermute | solution.py:42
  30.3 3.3 %collective-permute-done.10.refs_10_ = bf16[24,6144]{1,0:T(8,128)(2,1)S(1)} collective-permute-done((bf16[24,6144]{1,0:T(8,128)(2,1)S(1)}, bf16[24,6144]{1,0:T(8,128)(2,1)S(1)}, u32[]{:S(2)}, u32[]{:S(2)}) %collective-permute-start.10) | collective-permute-done | bytes 294944 | tf_op jit(solution)/shard_map/cond/branch_0_fun/ppermute | solution.py:33
  33.6 1.5 %collective-permute-start.12 = (bf16[24,6144]{1,0:T(8,128)(2,1)S(1)}, bf16[24,6144]{1,0:T(8,128)(2,1)S(1)}, u32[]{:S(2)}, u32[]{:S(2)}) collective-permute-start(bf16[24,6144]{1,0:T(8,128)(2,1)S(1)} %collective-permute-done.10.refs_10_), channel_id=1, source_target_pairs={{0,2},{1,3},{2,4},{3,5},{4,6},{5,7},{6,0},{7,1},{8,10},{9,11},{10,... | collective-permute-start | bytes 884744 | tf_op jit(solution)/shard_map/cond/branch_0_fun/ppermute | solution.py:33
  35.1 1.5 %collective-permute-start.13 = (bf16[24,6144]{1,0:T(8,128)(2,1)S(1)}, bf16[24,6144]{1,0:T(8,128)(2,1)S(1)}, u32[]{:S(2)}, u32[]{:S(2)}) collective-permute-start(bf16[24,6144]{1,0:T(8,128)(2,1)S(1)} %collective-permute-done.10.refs_10_), channel_id=1, source_target_pairs={{0,1},{1,0},{2,3},{3,2},{4,5},{5,4},{6,7},{7,6},{8,9},{9,8},{10,11... | collective-permute-start | bytes 884744 | tf_op jit(solution)/shard_map/cond/branch_0_fun/ppermute | solution.py:42
  36.6 3.3 %collective-permute-done.4.refs_3_ = bf16[24,6144]{1,0:T(8,128)(2,1)S(1)} collective-permute-done((bf16[24,6144]{1,0:T(8,128)(2,1)S(1)}, bf16[24,6144]{1,0:T(8,128)(2,1)S(1)}, u32[]{:S(2)}, u32[]{:S(2)}) %collective-permute-start.4) | collective-permute-done | bytes 294944 | tf_op jit(solution)/shard_map/cond/branch_0_fun/ppermute | solution.py:33
  39.9 2.0 %collective-permute-start.14 = (bf16[24,6144]{1,0:T(8,128)(2,1)S(1)}, bf16[24,6144]{1,0:T(8,128)(2,1)S(1)}, u32[]{:S(2)}, u32[]{:S(2)}) collective-permute-start(bf16[24,6144]{1,0:T(8,128)(2,1)S(1)} %collective-permute-done.9.refs_12_), channel_id=1, source_target_pairs={{0,6},{1,7},{2,0},{3,1},{4,2},{5,3},{6,4},{7,5},{8,14},{9,15},{10,... | collective-permute-start | bytes 884744 | tf_op jit(solution)/shard_map/cond/branch_0_fun/ppermute | solution.py:38
  41.8 1.5 %collective-permute-start.6 = (bf16[24,6144]{1,0:T(8,128)(2,1)S(1)}, bf16[24,6144]{1,0:T(8,128)(2,1)S(1)}, u32[]{:S(2)}, u32[]{:S(2)}) collective-permute-start(bf16[24,6144]{1,0:T(8,128)(2,1)S(1)} %collective-permute-done.4.refs_3_), channel_id=1, source_target_pairs={{0,1},{1,0},{2,3},{3,2},{4,5},{5,4},{6,7},{7,6},{8,9},{9,8},{10,11... | collective-permute-start | bytes 884744 | tf_op jit(solution)/shard_map/cond/branch_0_fun/ppermute | solution.py:42
  43.3 3.0 %collective-permute-done.12.refs_11_ = bf16[24,6144]{1,0:T(8,128)(2,1)S(1)} collective-permute-done((bf16[24,6144]{1,0:T(8,128)(2,1)S(1)}, bf16[24,6144]{1,0:T(8,128)(2,1)S(1)}, u32[]{:S(2)}, u32[]{:S(2)}) %collective-permute-start.12) | collective-permute-done | bytes 294944 | tf_op jit(solution)/shard_map/cond/branch_0_fun/ppermute | solution.py:33
  46.3 6.1 %collective-permute-done.14.refs_15_ = bf16[24,6144]{1,0:T(8,128)(2,1)S(1)} collective-permute-done((bf16[24,6144]{1,0:T(8,128)(2,1)S(1)}, bf16[24,6144]{1,0:T(8,128)(2,1)S(1)}, u32[]{:S(2)}, u32[]{:S(2)}) %collective-permute-start.14) | collective-permute-done | bytes 294944 | tf_op jit(solution)/shard_map/cond/branch_0_fun/ppermute | solution.py:38
  52.4 17.5 %forward.2 = (bf16[2,192,1536]{2,1,0:T(8,128)(2,1)S(1)}, bf16[2,192,6144]{2,1,0:T(8,128)(2,1)}) custom-call(bf16[24,6144]{1,0:T(8,128)(2,1)} %get-tuple-element.21.refs_0_, bf16[24,6144]{1,0:T(8,128)(2,1)S(1)} %collective-permute-done.refs_1_, bf16[24,6144]{1,0:T(8,128)(2,1)S(1)} %collective-permute-done.2.refs_2_, ...), custom_call_target="tpu_custom_call" | custom-call | flops 7247757312 | bytes 37748736 | tf_op jit(solution)/shard_map/cond/branch_0_fun/forward/pallas_call | solution.py:178
  70.4 11.6 %partial_sums.2 = (bf16[96,6144]{1,0:T(8,128)(2,1)S(1)}, bf16[96,6144]{1,0:T(8,128)(2,1)}) custom-call(bf16[2,192,1536]{2,1,0:T(8,128)(2,1)S(1)} %get-tuple-element.32.dpre_ref.right_ref.left_ref, bf16[6144,1536]{1,0:T(8,128)(2,1)} %get-tuple-element.26.refs_16_.w_in_ref.own_ref), custom_call_target="tpu_custom_call" | custom-call | flops 3623878656 | bytes 18874368 | tf_op jit(solution)/shard_map/cond/branch_0_fun/partial_sums/pallas_call | solution.py:221
  82.1 1.5 %collective-permute-start.15 = (bf16[96,6144]{1,0:T(8,128)(2,1)}, bf16[96,6144]{1,0:T(8,128)(2,1)}, u32[]{:S(2)}, u32[]{:S(2)}) collective-permute-start(bf16[96,6144]{1,0:T(8,128)(2,1)} %get-tuple-element.34), channel_id=1, source_target_pairs={{0,1},{1,0},{2,3},{3,2},{4,5},{5,4},{6,7},{7,6},{8,9},{9,8},{10,11... | collective-permute-start | bytes 3538952 | tf_op jit(solution)/shard_map/cond/branch_0_fun/ppermute | solution.py:42
  83.6 23.4 %finish.3 = bf16[6144,1536]{1,0:T(8,128)(2,1)} custom-call(f32[1]{0:T(128)} %bitcast.factor_ref, bf16[6144,1536]{1,0:T(8,128)(2,1)} %get-tuple-element.26.refs_16_.w_in_ref.own_ref, bf16[6144,1536]{1,0:T(8,128)(2,1)} %copy-done.10, bf16[2,192,6144]{2,1,0:T(8,128)(2,1)} %get-tuple-element.37.left_ref.right_ref, ...), custom_call_target="tpu_custom_call" | custom-call | flops 7247757312 | bytes 56623104 | tf_op jit(solution)/shard_map/cond/branch_0_fun/finish/pallas_call | solution.py:271
  107.0 3.8 %collective-permute-done.15 = bf16[96,6144]{1,0:T(8,128)(2,1)} collective-permute-done((bf16[96,6144]{1,0:T(8,128)(2,1)}, bf16[96,6144]{1,0:T(8,128)(2,1)}, u32[]{:S(2)}, u32[]{:S(2)}) %collective-permute-start.15) | collective-permute-done | bytes 1179680 | tf_op jit(solution)/shard_map/cond/branch_0_fun/ppermute | solution.py:42
  110.8 1.3 add_convert_fusion.1
  112.1 1.7 %collective-permute-start.18 = (bf16[24,6144]{1,0:T(8,128)(2,1)S(1)}, bf16[24,6144]{1,0:T(8,128)(2,1)S(1)}, u32[]{:S(2)}, u32[]{:S(2)}) collective-permute-start(bf16[24,6144]{1,0:T(8,128)(2,1)S(1)} %get-tuple-element.82), channel_id=1, source_target_pairs={{0,6},{1,7},{2,0},{3,1},{4,2},{5,3},{6,4},{7,5},{8,14},{9,15},{10,... | collective-permute-start | bytes 884744 | tf_op jit(solution)/shard_map/cond/branch_0_fun/ppermute | solution.py:103
  114.5 1.6 %collective-permute-start.20 = (bf16[24,6144]{1,0:T(8,128)(2,1)S(1)}, bf16[24,6144]{1,0:T(8,128)(2,1)S(1)}, u32[]{:S(2)}, u32[]{:S(2)}) collective-permute-start(bf16[24,6144]{1,0:T(8,128)(2,1)S(1)} %get-tuple-element.80), channel_id=1, source_target_pairs={{0,2},{1,3},{2,4},{3,5},{4,6},{5,7},{6,0},{7,1},{8,10},{9,11},{10,... | collective-permute-start | bytes 884744 | tf_op jit(solution)/shard_map/cond/branch_0_fun/ppermute | solution.py:103
  116.1 24.2 %finish.4 = bf16[1536,6144]{1,0:T(8,128)(2,1)} custom-call(f32[1]{0:T(128)} %bitcast.1.factor_ref, bf16[1536,6144]{1,0:T(8,128)(2,1)} %get-tuple-element.41.refs_17_.own_ref, bf16[1536,6144]{1,0:T(8,128)(2,1)} %collective-permute-done.21.other_ref, bf16[2,192,1536]{2,1,0:T(8,128)(2,1)S(1)} %get-tuple-element.32.dpre_ref.right_ref.left_ref, ...), custom_call_target="tpu_custom_call" | custom-call | flops 7247757312 | bytes 56623104 | tf_op jit(solution)/shard_map/cond/branch_0_fun/finish/pallas_call | solution.py:271
  140.4 1.2 fusion
  141.8 0.7 copy-done.15
  (23 shorter events, 2.5 us)
Async XLA Ops:
  1.3 42.0 %collective-permute-start.7 = (bf16[6144,1536]{1,0:T(8,128)(2,1)}, bf16[6144,1536]{1,0:T(8,128)(2,1)S(1)}, u32[]{:S(2)}, u32[]{:S(2)}) collective-permute-start(bf16[6144,1536]{1,0:T(8,128)(2,1)} %get-tuple-element.26.refs_16_.w_in_ref.own_ref), channel_id=1, source_target_pairs={{0,8},{8,0},{16,24},{24,16},{1,9},{9,1},{17,25},{25,17},{2,10},{10... | collective-permute-start | bytes 56623112 | tf_op jit(solution)/shard_map/cond/branch_0_fun/ppermute | solution.py:14
  1.9 12.7 %collective-permute-start = (bf16[24,6144]{1,0:T(8,128)(2,1)}, bf16[24,6144]{1,0:T(8,128)(2,1)S(1)}, u32[]{:S(2)}, u32[]{:S(2)}) collective-permute-start(bf16[24,6144]{1,0:T(8,128)(2,1)} %get-tuple-element.21.refs_0_), channel_id=1, source_target_pairs={{0,2},{1,3},{2,4},{3,5},{4,6},{5,7},{6,0},{7,1},{8,10},{9,11},{10,... | collective-permute-start | bytes 884744 | tf_op jit(solution)/shard_map/cond/branch_0_fun/ppermute | solution.py:33
  4.5 10.1 %collective-permute-start.1 = (bf16[24,6144]{1,0:T(8,128)(2,1)}, bf16[24,6144]{1,0:T(8,128)(2,1)S(1)}, u32[]{:S(2)}, u32[]{:S(2)}) collective-permute-start(bf16[24,6144]{1,0:T(8,128)(2,1)} %get-tuple-element.21.refs_0_), channel_id=1, source_target_pairs={{0,1},{1,0},{2,3},{3,2},{4,5},{5,4},{6,7},{7,6},{8,9},{9,8},{10,11... | collective-permute-start | bytes 884744 | tf_op jit(solution)/shard_map/cond/branch_0_fun/ppermute | solution.py:42
  6.0 14.9 %collective-permute-start.8 = (bf16[24,6144]{1,0:T(8,128)(2,1)}, bf16[24,6144]{1,0:T(8,128)(2,1)S(1)}, u32[]{:S(2)}, u32[]{:S(2)}) collective-permute-start(bf16[24,6144]{1,0:T(8,128)(2,1)} %get-tuple-element.27.refs_8_), channel_id=1, source_target_pairs={{0,2},{1,3},{2,4},{3,5},{4,6},{5,7},{6,0},{7,1},{8,10},{9,11},{10,... | collective-permute-start | bytes 884744 | tf_op jit(solution)/shard_map/cond/branch_0_fun/ppermute | solution.py:33
  7.6 13.4 %collective-permute-start.9 = (bf16[24,6144]{1,0:T(8,128)(2,1)}, bf16[24,6144]{1,0:T(8,128)(2,1)S(1)}, u32[]{:S(2)}, u32[]{:S(2)}) collective-permute-start(bf16[24,6144]{1,0:T(8,128)(2,1)} %get-tuple-element.27.refs_8_), channel_id=1, source_target_pairs={{0,1},{1,0},{2,3},{3,2},{4,5},{5,4},{6,7},{7,6},{8,9},{9,8},{10,11... | collective-permute-start | bytes 884744 | tf_op jit(solution)/shard_map/cond/branch_0_fun/ppermute | solution.py:42
  14.6 12.6 %collective-permute-start.2 = (bf16[24,6144]{1,0:T(8,128)(2,1)S(1)}, bf16[24,6144]{1,0:T(8,128)(2,1)S(1)}, u32[]{:S(2)}, u32[]{:S(2)}) collective-permute-start(bf16[24,6144]{1,0:T(8,128)(2,1)S(1)} %collective-permute-done.refs_1_), channel_id=1, source_target_pairs={{0,2},{1,3},{2,4},{3,5},{4,6},{5,7},{6,0},{7,1},{8,10},{9,11},{10,... | collective-permute-start | bytes 884744 | tf_op jit(solution)/shard_map/cond/branch_0_fun/ppermute | solution.py:33
  16.1 11.1 %collective-permute-start.3 = (bf16[24,6144]{1,0:T(8,128)(2,1)S(1)}, bf16[24,6144]{1,0:T(8,128)(2,1)S(1)}, u32[]{:S(2)}, u32[]{:S(2)}) collective-permute-start(bf16[24,6144]{1,0:T(8,128)(2,1)S(1)} %collective-permute-done.refs_1_), channel_id=1, source_target_pairs={{0,1},{1,0},{2,3},{3,2},{4,5},{5,4},{6,7},{7,6},{8,9},{9,8},{10,11... | collective-permute-start | bytes 884744 | tf_op jit(solution)/shard_map/cond/branch_0_fun/ppermute | solution.py:42
  20.9 12.6 %collective-permute-start.10 = (bf16[24,6144]{1,0:T(8,128)(2,1)S(1)}, bf16[24,6144]{1,0:T(8,128)(2,1)S(1)}, u32[]{:S(2)}, u32[]{:S(2)}) collective-permute-start(bf16[24,6144]{1,0:T(8,128)(2,1)S(1)} %collective-permute-done.8.refs_9_), channel_id=1, source_target_pairs={{0,2},{1,3},{2,4},{3,5},{4,6},{5,7},{6,0},{7,1},{8,10},{9,11},{10,... | collective-permute-start | bytes 884744 | tf_op jit(solution)/shard_map/cond/branch_0_fun/ppermute | solution.py:33
  22.5 11.1 %collective-permute-start.11 = (bf16[24,6144]{1,0:T(8,128)(2,1)S(1)}, bf16[24,6144]{1,0:T(8,128)(2,1)S(1)}, u32[]{:S(2)}, u32[]{:S(2)}) collective-permute-start(bf16[24,6144]{1,0:T(8,128)(2,1)S(1)} %collective-permute-done.8.refs_9_), channel_id=1, source_target_pairs={{0,1},{1,0},{2,3},{3,2},{4,5},{5,4},{6,7},{7,6},{8,9},{9,8},{10,11... | collective-permute-start | bytes 884744 | tf_op jit(solution)/shard_map/cond/branch_0_fun/ppermute | solution.py:42
  27.2 12.6 %collective-permute-start.4 = (bf16[24,6144]{1,0:T(8,128)(2,1)S(1)}, bf16[24,6144]{1,0:T(8,128)(2,1)S(1)}, u32[]{:S(2)}, u32[]{:S(2)}) collective-permute-start(bf16[24,6144]{1,0:T(8,128)(2,1)S(1)} %collective-permute-done.2.refs_2_), channel_id=1, source_target_pairs={{0,2},{1,3},{2,4},{3,5},{4,6},{5,7},{6,0},{7,1},{8,10},{9,11},{10,... | collective-permute-start | bytes 884744 | tf_op jit(solution)/shard_map/cond/branch_0_fun/ppermute | solution.py:33
  28.8 13.1 %collective-permute-start.5 = (bf16[24,6144]{1,0:T(8,128)(2,1)S(1)}, bf16[24,6144]{1,0:T(8,128)(2,1)S(1)}, u32[]{:S(2)}, u32[]{:S(2)}) collective-permute-start(bf16[24,6144]{1,0:T(8,128)(2,1)S(1)} %collective-permute-done.2.refs_2_), channel_id=1, source_target_pairs={{0,1},{1,0},{2,3},{3,2},{4,5},{5,4},{6,7},{7,6},{8,9},{9,8},{10,11... | collective-permute-start | bytes 884744 | tf_op jit(solution)/shard_map/cond/branch_0_fun/ppermute | solution.py:42
  33.6 12.7 %collective-permute-start.12 = (bf16[24,6144]{1,0:T(8,128)(2,1)S(1)}, bf16[24,6144]{1,0:T(8,128)(2,1)S(1)}, u32[]{:S(2)}, u32[]{:S(2)}) collective-permute-start(bf16[24,6144]{1,0:T(8,128)(2,1)S(1)} %collective-permute-done.10.refs_10_), channel_id=1, source_target_pairs={{0,2},{1,3},{2,4},{3,5},{4,6},{5,7},{6,0},{7,1},{8,10},{9,11},{10,... | collective-permute-start | bytes 884744 | tf_op jit(solution)/shard_map/cond/branch_0_fun/ppermute | solution.py:33
  35.1 11.2 %collective-permute-start.13 = (bf16[24,6144]{1,0:T(8,128)(2,1)S(1)}, bf16[24,6144]{1,0:T(8,128)(2,1)S(1)}, u32[]{:S(2)}, u32[]{:S(2)}) collective-permute-start(bf16[24,6144]{1,0:T(8,128)(2,1)S(1)} %collective-permute-done.10.refs_10_), channel_id=1, source_target_pairs={{0,1},{1,0},{2,3},{3,2},{4,5},{5,4},{6,7},{7,6},{8,9},{9,8},{10,11... | collective-permute-start | bytes 884744 | tf_op jit(solution)/shard_map/cond/branch_0_fun/ppermute | solution.py:42
  39.9 12.5 %collective-permute-start.14 = (bf16[24,6144]{1,0:T(8,128)(2,1)S(1)}, bf16[24,6144]{1,0:T(8,128)(2,1)S(1)}, u32[]{:S(2)}, u32[]{:S(2)}) collective-permute-start(bf16[24,6144]{1,0:T(8,128)(2,1)S(1)} %collective-permute-done.9.refs_12_), channel_id=1, source_target_pairs={{0,6},{1,7},{2,0},{3,1},{4,2},{5,3},{6,4},{7,5},{8,14},{9,15},{10,... | collective-permute-start | bytes 884744 | tf_op jit(solution)/shard_map/cond/branch_0_fun/ppermute | solution.py:38
  41.8 10.5 %collective-permute-start.6 = (bf16[24,6144]{1,0:T(8,128)(2,1)S(1)}, bf16[24,6144]{1,0:T(8,128)(2,1)S(1)}, u32[]{:S(2)}, u32[]{:S(2)}) collective-permute-start(bf16[24,6144]{1,0:T(8,128)(2,1)S(1)} %collective-permute-done.4.refs_3_), channel_id=1, source_target_pairs={{0,1},{1,0},{2,3},{3,2},{4,5},{5,4},{6,7},{7,6},{8,9},{9,8},{10,11... | collective-permute-start | bytes 884744 | tf_op jit(solution)/shard_map/cond/branch_0_fun/ppermute | solution.py:42
  43.3 9.0 %copy-start.10 = (bf16[6144,1536]{1,0:T(8,128)(2,1)}, bf16[6144,1536]{1,0:T(8,128)(2,1)S(1)}, u32[]{:S(2)}) copy-start(bf16[6144,1536]{1,0:T(8,128)(2,1)S(1)} %collective-permute-done.7.other_ref) | copy-start | bytes 56623108 | tf_op jit(solution)/shard_map/cond
  69.8 12.2 %collective-permute-start.16 = (bf16[2,192,6144]{2,1,0:T(8,128)(2,1)}, bf16[2,192,6144]{2,1,0:T(8,128)(2,1)}, u32[]{:S(2)}, u32[]{:S(2)}) collective-permute-start(bf16[2,192,6144]{2,1,0:T(8,128)(2,1)} %get-tuple-element.37.left_ref.right_ref), channel_id=1, source_target_pairs={{0,8},{8,0},{16,24},{24,16},{1,9},{9,1},{17,25},{25,17},{2,10},{10... | collective-permute-start | bytes 14155784 | tf_op jit(solution)/shard_map/cond/branch_0_fun/ppermute | solution.py:14
  69.9 12.1 %collective-permute-start.17 = (bf16[2,192,1536]{2,1,0:T(8,128)(2,1)S(1)}, bf16[2,192,1536]{2,1,0:T(8,128)(2,1)S(1)}, u32[]{:S(2)}, u32[]{:S(2)}) collective-permute-start(bf16[2,192,1536]{2,1,0:T(8,128)(2,1)S(1)} %get-tuple-element.32.dpre_ref.right_ref.left_ref), channel_id=1, source_target_pairs={{0,8},{8,0},{16,24},{24,16},{1,9},{9,1},{17,25},{25,17},{2,10},{10... | collective-permute-start | bytes 3538952 | tf_op jit(solution)/shard_map/cond/branch_0_fun/ppermute | solution.py:14
  82.0 34.1 %collective-permute-start.21 = (bf16[1536,6144]{1,0:T(8,128)(2,1)}, bf16[1536,6144]{1,0:T(8,128)(2,1)}, u32[]{:S(2)}, u32[]{:S(2)}) collective-permute-start(bf16[1536,6144]{1,0:T(8,128)(2,1)} %get-tuple-element.41.refs_17_.own_ref), channel_id=1, source_target_pairs={{0,8},{8,0},{16,24},{24,16},{1,9},{9,1},{17,25},{25,17},{2,10},{10... | collective-permute-start | bytes 56623112 | tf_op jit(solution)/shard_map/cond/branch_0_fun/ppermute | solution.py:14
  82.1 28.6 %collective-permute-start.15 = (bf16[96,6144]{1,0:T(8,128)(2,1)}, bf16[96,6144]{1,0:T(8,128)(2,1)}, u32[]{:S(2)}, u32[]{:S(2)}) collective-permute-start(bf16[96,6144]{1,0:T(8,128)(2,1)} %get-tuple-element.34), channel_id=1, source_target_pairs={{0,1},{1,0},{2,3},{3,2},{4,5},{5,4},{6,7},{7,6},{8,9},{9,8},{10,11... | collective-permute-start | bytes 3538952 | tf_op jit(solution)/shard_map/cond/branch_0_fun/ppermute | solution.py:42
  112.1 28.2 %collective-permute-start.18 = (bf16[24,6144]{1,0:T(8,128)(2,1)S(1)}, bf16[24,6144]{1,0:T(8,128)(2,1)S(1)}, u32[]{:S(2)}, u32[]{:S(2)}) collective-permute-start(bf16[24,6144]{1,0:T(8,128)(2,1)S(1)} %get-tuple-element.82), channel_id=1, source_target_pairs={{0,6},{1,7},{2,0},{3,1},{4,2},{5,3},{6,4},{7,5},{8,14},{9,15},{10,... | collective-permute-start | bytes 884744 | tf_op jit(solution)/shard_map/cond/branch_0_fun/ppermute | solution.py:103
  113.9 26.5 %collective-permute-start.19 = (bf16[24,6144]{1,0:T(8,128)(2,1)S(1)}, bf16[24,6144]{1,0:T(8,128)(2,1)S(1)}, u32[]{:S(2)}, u32[]{:S(2)}) collective-permute-start(bf16[24,6144]{1,0:T(8,128)(2,1)S(1)} %get-tuple-element.81), channel_id=1, source_target_pairs={{0,4},{1,5},{2,6},{3,7},{4,0},{5,1},{6,2},{7,3},{8,12},{9,13},{10,... | collective-permute-start | bytes 884744 | tf_op jit(solution)/shard_map/cond/branch_0_fun/ppermute | solution.py:103
  114.5 25.8 %collective-permute-start.20 = (bf16[24,6144]{1,0:T(8,128)(2,1)S(1)}, bf16[24,6144]{1,0:T(8,128)(2,1)S(1)}, u32[]{:S(2)}, u32[]{:S(2)}) collective-permute-start(bf16[24,6144]{1,0:T(8,128)(2,1)S(1)} %get-tuple-element.80), channel_id=1, source_target_pairs={{0,2},{1,3},{2,4},{3,5},{4,6},{5,7},{6,0},{7,1},{8,10},{9,11},{10,... | collective-permute-start | bytes 884744 | tf_op jit(solution)/shard_map/cond/branch_0_fun/ppermute | solution.py:103
  141.8 0.7 copy-start.15
